TPU v7x, 32 devices: a whole 2x2x4 slice. The times are simulated.
32 devices in a mesh: lm: 8 (over z, x), kf: 4 (over y, core).
Axes of the slice: x: 2, y: 2, z: 4, core: 2. Of those that a mesh axis runs over, the one named last changes fastest.
Arguments:
- residual_rows: bfloat16 [4096, 128], P(('lm', 'kf')), may hold values from -6 to 6
- jacobian: bfloat16 [4096, 15, 128], P(('lm', 'kf')), may hold values from -1.5 to 1.5
- nullspace: bfloat16 [4096, 128, 128], P(('lm', 'kf')), may hold values from -0.5 to 0.5
- frame_ids: int32 [4096, 64], P(('lm', 'kf')), may hold values from 0 to 16383, as said below
- obs_count: int32 [4096], P(('lm', 'kf')), may hold values from 4 to 64
- damping: float32 [15, 16384], P(None, 'kf'), may hold values from 1 to 10
- jacobi_scale: float32 [15, 16384], P(None, 'kf'), may hold values from 0.02 to 0.3
Outputs:
- solution: float32 [15, 16384], P(None, 'kf')
- residual: float32 [15, 16384], P(None, 'kf')
Inputs may be any that keep to these rules, and one draw needn't show every extreme that they name: `frame_ids`: within a block the keyframe ids rise strictly from slot to slot by 1 to 8. A block stored on the device with kf index w names only keyframes from 4096 * w up to but not including 4096 * (w + 2), and never one of 16384 or more.
All inputs are finite; a program needn't handle non-finite values.
Results may differ from a plain program's by a relative error of at most 0.005.
Values sent between devices are 32-bit elements; how exact they have to be, the bound alone decides.
A program may use at most 64 MiB of HBM per device.

v0:
```python
import jax
import jax.numpy as jnp
from jax import lax
from jax.sharding import PartitionSpec as P

ITERS = 2


def passed_along(array, axis, by):
    length = lax.axis_size(axis)
    pairs = [(i, i + by) for i in range(length) if 0 <= i + by < length]
    return lax.ppermute(array, axis, pairs)


def row_layout(frame_ids, obs_count, first_frame):
    slots = lax.broadcasted_iota(jnp.int32, frame_ids.shape, 1)
    live = (slots < obs_count[:, None]).astype(jnp.float32)
    return (jnp.repeat(frame_ids - first_frame, 2, axis=1), jnp.repeat(live, 2, axis=1))


def project(lifted, nullspace, live):
    lifted_half = (lifted * live).astype(jnp.bfloat16)
    inner = jnp.einsum(
        "brk,br->bk", nullspace, lifted_half, preferred_element_type=jnp.float32
    ).astype(jnp.bfloat16)
    spread = jnp.einsum("brk,bk->br", nullspace, inner, preferred_element_type=jnp.float32)
    return spread * live


def spread_back(spread, jacobian, row_ids, width):
    terms = jacobian * spread[:, None, :]
    terms = jnp.moveaxis(terms, 1, 0).reshape(jacobian.shape[1], -1)
    return jnp.zeros((jacobian.shape[1], width), jnp.float32).at[:, row_ids.reshape(-1)].add(terms)


def window_pair(field):
    return jnp.concatenate([field, passed_along(field, "kf", -1)], axis=1)


def fold_next(partial_value, frames):
    return partial_value[:, :frames] + passed_along(partial_value[:, frames:], "kf", 1)


def inner_window(left, right):
    return lax.psum(jnp.sum(left * right), "kf")


def shards(residual_rows, jacobian, nullspace, frame_ids, obs_count, damping, jacobi_scale):
    frames = damping.shape[1]
    row_ids, live = row_layout(frame_ids, obs_count, lax.axis_index("kf") * frames)

    def local_terms(window_field):
        if window_field is None:
            lifted = residual_rows.astype(jnp.float32)
        else:
            gathered = jnp.take(window_field, row_ids, axis=1)
            lifted = jnp.sum(jacobian * jnp.moveaxis(gathered, 0, 1), axis=1)
        return spread_back(project(lifted, nullspace, live), jacobian, row_ids, 2 * frames)

    def combine(partial_value):
        return lax.psum(fold_next(partial_value, frames), "lm")

    damp_part, scale_part = (damping, jacobi_scale)
    gradient = -combine(local_terms(None))
    residual = gradient
    solution = jnp.zeros_like(gradient)
    scaled = scale_part * residual
    direction = scaled
    energy = inner_window(residual, scaled)
    for step_index in range(ITERS):
        applied = combine(local_terms(window_pair(direction))) + damp_part * direction
        step_size = energy / inner_window(direction, applied)
        solution = solution + step_size * direction
        residual = residual - step_size * applied
        if step_index + 1 < ITERS:
            scaled = scale_part * residual
            fresh = inner_window(residual, scaled)
            direction = scaled + fresh / energy * direction
            energy = fresh
    return (solution, residual)


def solution(mesh):
    placed = (
        P(("lm", "kf"), None),
        P(("lm", "kf"), None, None),
        P(("lm", "kf"), None, None),
        P(("lm", "kf"), None),
        P(("lm", "kf")),
        P(None, "kf"),
        P(None, "kf"),
    )
    return jax.shard_map(
        shards,
        mesh=mesh,
        in_specs=placed,
        out_specs=(P(None, "kf"), P(None, "kf")),
        check_vma=False,
    )
```

profile of v0, /device:TPU:0, one launch (start us, length us, event | category | flops | bytes accessed | tf_op | source)
XLA Modules:
  0.0 765.3 jit_solution(5595085198218443961)
XLA Ops:
  15.1 4.3 broadcast_in_dim.13.clone
  19.4 5.5 reshape_reshape.2
  25.1 4.7 copy.161
  29.8 89.9 %scatter_custom_fusion = f32[15,8192]{0,1:T(8,128)} fusion(s32[16384]{0:T(1024)S(1)} %bitcast.77, f32[16384,15]{1,0:T(8,128)} %bitcast.65, f32[]{:T(128)} %constant.1.clone.1), kind=kCustom, calls=%fused_computation.9 | custom fusion | flops 245760 | bytes 492032 | tf_op jit(solution)/shard_map/scatter-add | solution.py:33
  119.6 3.8 fusion.27
  132.5 77.6 %all-reduce.5.cloned.1.call-done = f32[15,4096]{1,0:T(8,128)} async-done(((f32[15,4096]{1,0:T(8,128)}), f32[15,4096]{1,0:T(8,128)}) %all-reduce.5.cloned.1.call-update) | async-done | bytes 245776 | tf_op jit(solution)/shard_map/psum | solution.py:61
  217.2 56.6 %gather_fusion = f32[16384,15]{1,0:T(8,128)} fusion(f32[15,8192]{0,1:T(8,128)} %copy.133, s32[16384]{0:T(1024)S(1)} %bitcast_clamp_fusion), kind=kCustom, calls=%fused_computation.clone | custom fusion | bytes 2031616 | tf_op jit(solution)/shard_map/jit(_take)/gather | solution.py:56
  273.8 5.3 copy.134
  279.3 3.5 fusion.17
  285.4 4.7 copy.162
  290.1 89.9 %scatter_custom_fusion.1 = f32[15,8192]{0,1:T(8,128)} fusion(s32[16384]{0:T(1024)S(1)} %bitcast.78, f32[16384,15]{1,0:T(8,128)} %bitcast.66, f32[]{:T(128)} %constant.1.clone.1), kind=kCustom, calls=%fused_computation.7 | custom fusion | flops 245760 | bytes 492032 | tf_op jit(solution)/shard_map/scatter-add | solution.py:33
  380.0 3.8 fusion.26
  386.8 6.7 collective-permute-start.2
  396.7 72.9 %all-reduce.7.cloned.1.call-done = f32[15,4096]{1,0:T(8,128)} async-done(((f32[15,4096]{1,0:T(8,128)}), f32[15,4096]{1,0:T(8,128)}) %all-reduce.7.cloned.1.call-update) | async-done | bytes 245776 | tf_op jit(solution)/shard_map/psum | solution.py:61
  471.2 6.3 all-reduce
  481.3 7.2 psum.53
  496.0 56.6 %gather_fusion.1 = f32[16384,15]{1,0:T(8,128)} fusion(f32[15,8192]{0,1:T(8,128)} %copy.142, s32[16384]{0:T(1024)S(1)} %bitcast_clamp_fusion), kind=kCustom, calls=%fused_computation.1.clone | custom fusion | bytes 2031616 | tf_op jit(solution)/shard_map/jit(_take)/gather | solution.py:56
  552.6 5.4 copy.143
  564.3 4.7 copy.163
  569.0 89.9 %scatter_custom_fusion.2 = f32[15,8192]{0,1:T(8,128)} fusion(s32[16384]{0:T(1024)} %bitcast.79, f32[16384,15]{1,0:T(8,128)} %bitcast.64, f32[]{:T(128)} %constant.1.clone.1), kind=kCustom, calls=%fused_computation.5 | custom fusion | flops 245760 | bytes 492032 | tf_op jit(solution)/shard_map/scatter-add | solution.py:33
  658.8 3.8 fusion.25
  665.6 6.1 collective-permute-start.4
  674.9 72.9 %all-reduce.9.cloned.1.call-done = f32[15,4096]{1,0:T(8,128)} async-done(((f32[15,4096]{1,0:T(8,128)}), f32[15,4096]{1,0:T(8,128)}) %all-reduce.9.cloned.1.call-update) | async-done | bytes 245776 | tf_op jit(solution)/shard_map/psum | solution.py:61
  749.4 6.3 psum.55
  (96 shorter events, 58.9 us)
Async XLA Ops:
  7.2 202.9 %all-reduce.5.cloned.1.call-start = ((), (), s32[]{:S(2)}) async-start(), calls=%async_computation | async-start | bytes 524288 | tf_op jit(solution)/shard_map/psum | solution.py:61
  8.9 3.6 copy-start
  8.9 6.0 copy-start.11
  15.1 9.9 %copy-start.3 = (bf16[128,15,128]{2,0,1:T(8,128)(2,1)S(1)}, bf16[128,15,128]{2,0,1:T(8,128)(2,1)}, u32[]{:S(2)}) copy-start(bf16[128,15,128]{2,0,1:T(8,128)(2,1)} %param.10) | copy-start | bytes 1474564
  25.0 265.1 %copy-start.10 = (s32[16384,1]{0,1:T(1,128)}, s32[16384,1]{0,1:T(1,128)S(1)}, u32[]{:S(2)}) copy-start(s32[16384,1]{0,1:T(1,128)S(1)} %compare_select_fusion) | copy-start | bytes 196612
  123.5 86.6 %copy-start.6 = (f32[15,4096]{1,0:T(8,128)S(1)}, f32[15,4096]{1,0:T(8,128)}, u32[]{:S(2)}) copy-start(f32[15,4096]{1,0:T(8,128)} %param.15) | copy-start | bytes 737284
  126.4 3.9 collective-permute-start
  132.0 337.5 %all-reduce.7.cloned.1.call-start = ((), (), s32[]{:S(2)}) async-start(), calls=%async_computation.1 | async-start | bytes 524288 | tf_op jit(solution)/shard_map/psum | solution.py:61
  132.2 147.0 %copy-start.8 = (f32[128,128]{1,0:T(8,128)}, f32[128,128]{1,0:T(8,128)S(1)}, u32[]{:S(2)}) copy-start(f32[128,128]{1,0:T(8,128)S(1)} %copy.135) | copy-start | bytes 196612
  211.0 3.4 collective-permute-start.1
  279.1 3.7 copy-start.1
  383.8 85.7 %copy-start.4 = (f32[15,4096]{1,0:T(8,128)S(1)}, f32[15,4096]{1,0:T(8,128)}, u32[]{:S(2)}) copy-start(f32[15,4096]{1,0:T(8,128)} %param.14) | copy-start | bytes 737284
  383.8 85.7 %copy-start.5 = (f32[15,4096]{1,0:T(8,128)S(1)}, f32[15,4096]{1,0:T(8,128)}, u32[]{:S(2)}) copy-start(f32[15,4096]{1,0:T(8,128)} %all-reduce.5.cloned.1.call-done) | copy-start | bytes 737284
  386.8 8.0 %collective-permute-start.2 = (f32[15,4096]{1,0:T(8,128)}, f32[15,4096]{1,0:T(8,128)}, u32[]{:S(2)}, u32[]{:S(2)}) collective-permute-start(f32[15,4096]{1,0:T(8,128)} %copy.139), channel_id=1, source_target_pairs={{0,1},{1,2},{2,3},{4,5},{5,6},{6,7},{8,9},{9,10},{10,11},{12,13},{... | collective-permute-start | bytes 737288 | tf_op jit(solution)/shard_map/ppermute | solution.py:12
  396.6 351.2 %all-reduce.9.cloned.1.call-start = ((), (), s32[]{:S(2)}) async-start(), calls=%async_computation.2 | async-start | bytes 524288 | tf_op jit(solution)/shard_map/psum | solution.py:61
  489.8 3.4 collective-permute-start.3
  552.6 5.5 copy-start.9
  557.9 3.7 copy-start.2
  662.7 94.3 %copy-start.7 = (f32[15,4096]{1,0:T(8,128)S(1)}, f32[15,4096]{1,0:T(8,128)}, u32[]{:S(2)}) copy-start(f32[15,4096]{1,0:T(8,128)} %get-tuple-element.19) | copy-start | bytes 737284
  665.6 7.5 collective-permute-start.4
Sparse Core Ops, SparseCore 0:
  132.2 77.8 all-reduce.4
  396.7 72.7 all-reduce.6
  675.0 72.7 all-reduce.8
where the time goes:
time: 766 us; the launch traced here: 765 us
  other arithmetic  285 us (37%)
  waiting for transfers between devices  227 us (30%)
  local copies, waits for them, and re-layouts  179 us (23%)
  blocking collectives  19.8 us (3%)
  starting transfers between devices  19 us (2%)
  between operations  18.1 us (2%)
  matrix products  17.3 us (2%)
    scatter-add x3, other arithmetic, spread_back(): jnp.zeros((jacobian.shape[1], width), jnp.float32)  270 us
    psum x3, waiting for transfers between devices, combine(): return lax.psum(fold_next(partial_value, frames), 'lm')  223 us
    gather x4, local copies, waits for them, and re-layouts, local_terms(): gathered = jnp.take(window_field, row_ids, axis=1)  124 us
    slice x6, local copies, waits for them, and re-layouts, fold_next(): partial_value[:, frames:]  20.4 us
    psum x3, blocking collectives, inner_window(): return lax.psum(jnp.sum(left * right), 'kf')  19.8 us
    ppermute x5, starting transfers between devices, passed_along(): return lax.ppermute(array, axis, pairs)  18.9 us
  transfers between devices with their start and end apart: 8, of which 6 were waited for; matrix products, arithmetic and copies ran while one was open for 0% of the time, Pallas kernels for 0%

commit v1 on v0

v1 whole, which is shorter than its diff:
```python
import functools

import jax
import jax.numpy as jnp
from jax import lax
from jax.experimental import pallas as pl
from jax.experimental.pallas import tpu as pltpu
from jax.sharding import PartitionSpec as P

ITERS = 2
LANES = 128
PAD = 16
SPAN = 5
CHUNK = 16


def local_kernel(use_field, starts, field_ref, code_ref, res_ref, jac_ref, null_ref, out_ref):
    step = pl.program_id(0)

    @pl.when(step == 0)
    def _():
        out_ref[...] = jnp.zeros_like(out_ref)

    lane_iota = lax.broadcasted_iota(jnp.int32, (LANES, LANES), 0)

    def one(i):
        start = starts[step * CHUNK + i]
        code = code_ref[pl.ds(i, 1), :]
        part = code >> 7
        hot = jnp.where(lane_iota == (code & (LANES - 1)), 1.0, 0.0).astype(jnp.bfloat16)
        jac = jac_ref[i].astype(jnp.float32)
        null = null_ref[i]
        if use_field:
            window = field_ref[pl.ds(start, SPAN)].reshape(SPAN * PAD, LANES).astype(jnp.bfloat16)
            spots = jnp.dot(window, hot, preferred_element_type=jnp.float32)
            gathered = jnp.zeros((PAD, LANES), jnp.float32)
            for q in range(SPAN):
                gathered = jnp.where(part == q, spots[q * PAD:(q + 1) * PAD], gathered)
            lifted = jnp.sum(jac * gathered, axis=0, keepdims=True)
        else:
            lifted = jnp.where(code >= 0, res_ref[pl.ds(i, 1), :], 0.0)
        inner = jnp.dot(
            lifted.astype(jnp.bfloat16), null, preferred_element_type=jnp.float32
        ).astype(jnp.bfloat16)
        spread = lax.dot_general(
            inner, null, (((1,), (1,)), ((), ())), preferred_element_type=jnp.float32
        )
        terms = jac * spread
        placed = jnp.concatenate(
            [jnp.where(part == q, terms, 0.0) for q in range(SPAN)], axis=0
        ).astype(jnp.bfloat16)
        back = lax.dot_general(
            placed, hot, (((1,), (1,)), ((), ())), preferred_element_type=jnp.float32
        )
        return start, back.reshape(SPAN, PAD, LANES)

    for i in range(CHUNK):
        start, back = one(i)
        out_ref[pl.ds(start, SPAN)] += back


def local_terms(use_field, starts, field, code, res, jac, null):
    blocks = null.shape[0]
    groups = field.shape[0]
    return pl.pallas_call(
        functools.partial(local_kernel, use_field),
        grid_spec=pltpu.PrefetchScalarGridSpec(
            num_scalar_prefetch=1,
            grid=(blocks // CHUNK,),
            in_specs=[
                pl.BlockSpec(field.shape, lambda b, s: (0, 0, 0)),
                pl.BlockSpec((CHUNK, LANES), lambda b, s: (b, 0)),
                pl.BlockSpec((CHUNK, LANES), lambda b, s: (b, 0)),
                pl.BlockSpec((CHUNK, PAD, LANES), lambda b, s: (b, 0, 0)),
                pl.BlockSpec((CHUNK, LANES, LANES), lambda b, s: (b, 0, 0)),
            ],
            out_specs=pl.BlockSpec((groups, PAD, LANES), lambda b, s: (0, 0, 0)),
        ),
        out_shape=jax.ShapeDtypeStruct((groups, PAD, LANES), jnp.float32),
        name="local_field" if use_field else "local_gradient",
    )(starts, field, code, res, jac, null)


def passed_along(array, axis, by):
    length = lax.axis_size(axis)
    pairs = [(i, i + by) for i in range(length) if 0 <= i + by < length]
    return lax.ppermute(array, axis, pairs)


def to_groups(array):
    state, frames = array.shape
    padded = jnp.pad(array, ((0, PAD - state), (0, 0)))
    return jnp.moveaxis(padded.reshape(PAD, frames // LANES, LANES), 1, 0)


def from_groups(array, state):
    return jnp.moveaxis(array, 0, 1).reshape(PAD, -1)[:state]


def prepare(frame_ids, obs_count, first_frame, groups):
    rel = frame_ids - first_frame
    starts = jnp.minimum(rel[:, 0] // LANES, groups - SPAN)
    slots = lax.broadcasted_iota(jnp.int32, rel.shape, 1)
    off = jnp.where(slots < obs_count[:, None], rel - starts[:, None] * LANES, -1)
    twice = (
        lax.broadcasted_iota(jnp.int32, (rel.shape[1], 2 * rel.shape[1]), 0)
        == lax.broadcasted_iota(jnp.int32, (rel.shape[1], 2 * rel.shape[1]), 1) // 2
    ).astype(jnp.float32)
    code = jnp.dot(off.astype(jnp.float32), twice, precision=lax.Precision.HIGHEST)
    return starts, jnp.round(code).astype(jnp.int32)


def shards(residual_rows, jacobian, nullspace, frame_ids, obs_count, damping, jacobi_scale):
    state, frames = damping.shape
    own = frames // LANES
    starts, code = prepare(frame_ids, obs_count, lax.axis_index("kf") * frames, 2 * own)
    jac = jnp.pad(jacobian, ((0, 0), (0, PAD - state), (0, 0)))
    res = residual_rows.astype(jnp.float32)
    damp, scale = to_groups(damping), to_groups(jacobi_scale)

    def product(field):
        if field is None:
            pair = jnp.zeros((2 * own, PAD, LANES), jnp.float32)
        else:
            pair = jnp.concatenate([field, passed_along(field, "kf", -1)], axis=0)
        total = local_terms(field is not None, starts, pair, code, res, jac, nullspace)
        return lax.psum(total[:own] + passed_along(total[own:], "kf", 1), "lm")

    def inner_window(left, right):
        return lax.psum(jnp.sum(left * right), "kf")

    residual = -product(None)
    direction = scale * residual
    energy = inner_window(residual, direction)
    answer = jnp.zeros_like(residual)
    for step_index in range(ITERS):
        applied = product(direction) + damp * direction
        step_size = energy / inner_window(direction, applied)
        answer = answer + step_size * direction
        residual = residual - step_size * applied
        if step_index + 1 < ITERS:
            scaled = scale * residual
            fresh = inner_window(residual, scaled)
            direction = scaled + fresh / energy * direction
            energy = fresh
    return (from_groups(answer, state), from_groups(residual, state))


def solution(mesh):
    placed = (
        P(("lm", "kf"), None),
        P(("lm", "kf"), None, None),
        P(("lm", "kf"), None, None),
        P(("lm", "kf"), None),
        P(("lm", "kf")),
        P(None, "kf"),
        P(None, "kf"),
    )
    return jax.shard_map(
        shards,
        mesh=mesh,
        in_specs=placed,
        out_specs=(P(None, "kf"), P(None, "kf")),
        check_vma=False,
    )
```

time: 766 us -> 418 us (0.55)
  other arithmetic: 285 us -> 16.5 us
  local copies, waits for them, and re-layouts: 179 us -> 7.92 us
  Pallas kernels: 0 us -> 104 us
  matrix products: 17.3 us -> 1.58 us
    scatter-add x3 -> x0, other arithmetic: 270 us -> none  [spread_back(): jnp.zeros((jacobian.shape[1], width), jnp.float32)]
    gather x4 -> x0, local copies, waits for them, and re-layouts: 124 us -> none  [local_terms(): gathered = jnp.take(window_field, row_ids, axis=1)]
    pallas_call x0 -> x3, Pallas kernels: none -> 104 us  [local_terms(): pl.pallas_call(functools.partial(local_kernel, use_field), grid_spec=pltp...]
    slice x6 -> x5, local copies, waits for them, and re-layouts: 20.4 us -> 3.06 us  [the longest x3 2.9 us: product(): return lax.psum(total[:own] + passed_along(total[own:], 'kf', 1), 'lm')]
    dot_general x6 -> x1, matrix products: 17.3 us -> 1.58 us  [prepare(): jnp.dot(off.astype(jnp.float32), twice, precision=lax.Precision.HIGHEST)]
    reshape x4 -> x0, local copies, waits for them, and re-layouts: 14.1 us -> none  [the longest x3 14.1 us: spread_back(): terms = jnp.moveaxis(terms, 1, 0).reshape(jacobian.shape[1], -1)]
  transfers between devices with their start and end apart: 8 -> 8, of which waited for: 6 -> 8; matrix products, arithmetic and copies ran while one was open for 0% -> 0% of each run, Pallas kernels for 0% -> 0%
where the time goes in v1:
time: 418 us; the launch traced here: 417 us
  waiting for transfers between devices  233 us (56%)
  Pallas kernels  104 us (25%)
  blocking collectives  19.8 us (5%)
  between operations  17.8 us (4%)
  starting transfers between devices  16.7 us (4%)
  other arithmetic  16.5 us (4%)
  local copies, waits for them, and re-layouts  7.92 us (2%)
    psum x3, waiting for transfers between devices, product(): return lax.psum(total[:own] + passed_along(total[own:], 'kf', 1), 'lm')  225 us
    pallas_call x3, Pallas kernels, local_terms(): pl.pallas_call(functools.partial(local_kernel, use_field), grid_spec=pltp...  104 us
    psum x3, blocking collectives, inner_window(): return lax.psum(jnp.sum(left * right), 'kf')  19.8 us
    ppermute x5, starting transfers between devices, passed_along(): return lax.ppermute(array, axis, pairs)  16.6 us
  transfers between devices with their start and end apart: 8, of which 8 were waited for; matrix products, arithmetic and copies ran while one was open for 0% of the time, Pallas kernels for 0%

profile of v1, /device:TPU:0, one launch (start us, length us, event | category | flops | bytes accessed | tf_op | source)
XLA Modules:
  0.0 417.2 jit_solution(6695165731884354592)
XLA Ops:
  8.6 1.4 convert_element_type.17.res_ref
  10.0 1.4 copy.10
  12.2 1.6 fusion.code_ref
  14.7 24.3 %local_gradient.1 = f32[64,16,128]{2,1,0:T(8,128)} custom-call(s32[128]{0:T(128)} %fusion.16.starts, f32[64,16,128]{2,1,0:T(8,128)} %broadcast_in_dim.9.field_ref, s32[128,128]{1,0:T(8,128)} %fusion.code_ref, f32[128,128]{1,0:T(8,128)} %convert_element_type.17.res_ref, bf16[128,16,128]{2,1,0:T(8,128)(2,1)} %pad.11.jac_ref, bf16[128,128,128]{2,1,0:T(8,128)(2,1)} %null_ref.5), custom_call_target="tpu_custom_call" | custom-call | tf_op jit(solution)/shard_map/local_gradient/pallas_call | solution.py:65
  39.9 2.4 collective-permute-start
  43.5 1.7 slice_add_fusion.2
  45.2 78.0 %all-reduce.8.cloned.1.call-done = f32[32,16,128]{2,1,0:T(8,128)} async-done(((f32[32,16,128]{2,1,0:T(8,128)}), f32[32,16,128]{2,1,0:T(8,128)}) %all-reduce.8.cloned.1.call-update) | async-done | bytes 262160 | tf_op jit(solution)/shard_map/psum | solution.py:127
  124.2 1.4 collective-permute-start.1
  125.7 2.1 collective-permute-done.1
  128.6 40.0 %local_field.2 = f32[64,16,128]{2,1,0:T(8,128)} custom-call(s32[128]{0:T(128)} %fusion.16.starts, f32[64,16,128]{2,1,0:T(8,128)} %pad_maximum_fusion.field_ref, s32[128,128]{1,0:T(8,128)} %fusion.code_ref, f32[128,128]{1,0:T(8,128)} %convert_element_type.17.res_ref, bf16[128,16,128]{2,1,0:T(8,128)(2,1)} %pad.11.jac_ref, bf16[128,128,128]{2,1,0:T(8,128)(2,1)} %null_ref.5), custom_call_target="tpu_custom_call" | custom-call | tf_op jit(solution)/shard_map/local_field/pallas_call | solution.py:65
  169.6 6.0 %collective-permute-start.2 = (f32[32,16,128]{2,1,0:T(8,128)S(1)}, f32[32,16,128]{2,1,0:T(8,128)S(1)}, u32[]{:S(2)}, u32[]{:S(2)}) collective-permute-start(f32[32,16,128]{2,1,0:T(8,128)S(1)} %slice.48), channel_id=1, source_target_pairs={{0,1},{1,2},{2,3},{4,5},{5,6},{6,7},{8,9},{9,10},{10,11},{12,13},{... | collective-permute-start | bytes 786440 | tf_op jit(solution)/shard_map/ppermute | solution.py:87
  176.8 1.7 slice_add_fusion.1
  178.5 73.5 %all-reduce.10.cloned.1.call-done = f32[32,16,128]{2,1,0:T(8,128)} async-done(((f32[32,16,128]{2,1,0:T(8,128)}), f32[32,16,128]{2,1,0:T(8,128)}) %all-reduce.10.cloned.1.call-update) | async-done | bytes 262160 | tf_op jit(solution)/shard_map/psum | solution.py:127
  252.0 1.7 multiply_reduce_fusion.2
  253.6 6.3 %all-reduce.3 = (f32[]{:T(128)}, f32[]{:T(128)}) all-reduce(f32[]{:T(128)} %get-tuple-element.3, f32[]{:T(128)} %get-tuple-element.2), channel_id=1, replica_groups=mesh['lm'=8,'kf'=4] {'kf'}, use_global_device_ids=true, to_apply=%region_2.3 | all-reduce | flops 2 | bytes 16 | tf_op jit(solution)/shard_map/psum | solution.py:130
  261.3 1.6 multiply_reduce_fusion.1
  262.9 7.2 %psum.53 = f32[]{:T(128)} all-reduce(f32[]{:T(128)} %get-tuple-element.6), channel_id=1, replica_groups=mesh['lm'=8,'kf'=4] {'kf'}, use_global_device_ids=true, to_apply=%region_7.8 | all-reduce | flops 1 | bytes 8 | tf_op jit(solution)/shard_map/psum | solution.py:130
  272.8 2.1 collective-permute-done.3
  275.8 40.0 %local_field.3 = f32[64,16,128]{2,1,0:T(8,128)} custom-call(s32[128]{0:T(128)} %fusion.16.starts, f32[64,16,128]{2,1,0:T(8,128)} %pad_maximum_fusion.1.field_ref, s32[128,128]{1,0:T(8,128)} %fusion.code_ref, f32[128,128]{1,0:T(8,128)} %convert_element_type.17.res_ref, bf16[128,16,128]{2,1,0:T(8,128)(2,1)} %pad.11.jac_ref, bf16[128,128,128]{2,1,0:T(8,128)(2,1)} %null_ref.5), custom_call_target="tpu_custom_call" | custom-call | tf_op jit(solution)/shard_map/local_field/pallas_call | solution.py:65
  316.7 5.5 %collective-permute-start.4 = (f32[32,16,128]{2,1,0:T(8,128)S(1)}, f32[32,16,128]{2,1,0:T(8,128)S(1)}, u32[]{:S(2)}, u32[]{:S(2)}) collective-permute-start(f32[32,16,128]{2,1,0:T(8,128)S(1)} %slice.50), channel_id=1, source_target_pairs={{0,1},{1,2},{2,3},{4,5},{5,6},{6,7},{8,9},{9,10},{10,11},{12,13},{... | collective-permute-start | bytes 786440 | tf_op jit(solution)/shard_map/ppermute | solution.py:87
  323.3 1.7 slice_add_fusion
  325.0 73.5 %all-reduce.12.cloned.1.call-done = f32[32,16,128]{2,1,0:T(8,128)} async-done(((f32[32,16,128]{2,1,0:T(8,128)}), f32[32,16,128]{2,1,0:T(8,128)}) %all-reduce.12.cloned.1.call-update) | async-done | bytes 262160 | tf_op jit(solution)/shard_map/psum | solution.py:127
  398.5 1.6 multiply_reduce_fusion
  400.1 6.3 %psum.55 = f32[]{:T(128)} all-reduce(f32[]{:T(128)} %multiply_reduce_fusion), channel_id=1, replica_groups=mesh['lm'=8,'kf'=4] {'kf'}, use_global_device_ids=true, to_apply=%region_10.11 | all-reduce | flops 1 | bytes 8 | tf_op jit(solution)/shard_map/psum | solution.py:130
  (37 shorter events, 16.5 us)
Async XLA Ops:
  7.2 116.1 %all-reduce.8.cloned.1.call-start = ((), (), s32[]{:S(2)}) async-start(), calls=%async_computation | async-start | bytes 524288 | tf_op jit(solution)/shard_map/psum | solution.py:127
  12.2 111.0 %copy-start.2 = (f32[15,4096]{1,0:T(8,128)S(1)}, f32[15,4096]{1,0:T(8,128)}, u32[]{:S(2)}) copy-start(f32[15,4096]{1,0:T(8,128)} %param.13) | copy-start | bytes 737284
  39.9 3.5 collective-permute-start
  45.2 206.8 %all-reduce.10.cloned.1.call-start = ((), (), s32[]{:S(2)}) async-start(), calls=%async_computation.1 | async-start | bytes 524288 | tf_op jit(solution)/shard_map/psum | solution.py:127
  124.2 127.8 %copy-start = (f32[15,4096]{1,0:T(8,128)S(1)}, f32[15,4096]{1,0:T(8,128)}, u32[]{:S(2)}) copy-start(f32[15,4096]{1,0:T(8,128)} %param.12) | copy-start | bytes 737284
  124.2 127.8 %copy-start.1 = (f32[32,16,128]{2,1,0:T(8,128)S(1)}, f32[32,16,128]{2,1,0:T(8,128)}, u32[]{:S(2)}) copy-start(f32[32,16,128]{2,1,0:T(8,128)} %all-reduce.8.cloned.1.call-done) | copy-start | bytes 786436
  124.2 3.6 collective-permute-start.1
  169.6 7.2 %collective-permute-start.2 = (f32[32,16,128]{2,1,0:T(8,128)S(1)}, f32[32,16,128]{2,1,0:T(8,128)S(1)}, u32[]{:S(2)}, u32[]{:S(2)}) collective-permute-start(f32[32,16,128]{2,1,0:T(8,128)S(1)} %slice.48), channel_id=1, source_target_pairs={{0,1},{1,2},{2,3},{4,5},{5,6},{6,7},{8,9},{9,10},{10,11},{12,13},{... | collective-permute-start | bytes 786440 | tf_op jit(solution)/shard_map/ppermute | solution.py:87
  178.5 220.0 %all-reduce.12.cloned.1.call-start = ((), (), s32[]{:S(2)}) async-start(), calls=%async_computation.2 | async-start | bytes 524288 | tf_op jit(solution)/shard_map/psum | solution.py:127
  271.5 3.4 collective-permute-start.3
  316.7 6.6 %collective-permute-start.4 = (f32[32,16,128]{2,1,0:T(8,128)S(1)}, f32[32,16,128]{2,1,0:T(8,128)S(1)}, u32[]{:S(2)}, u32[]{:S(2)}) collective-permute-start(f32[32,16,128]{2,1,0:T(8,128)S(1)} %slice.50), channel_id=1, source_target_pairs={{0,1},{1,2},{2,3},{4,5},{5,6},{6,7},{8,9},{9,10},{10,11},{12,13},{... | collective-permute-start | bytes 786440 | tf_op jit(solution)/shard_map/ppermute | solution.py:87
Sparse Core Ops, SparseCore 0:
  45.3 77.8 all-reduce.7
  178.6 73.3 all-reduce.9
  325.2 73.3 all-reduce.11

commit v2 on v1

--- a/solution.py
+++ b/solution.py
@@ -87,6 +87,208 @@
     return lax.ppermute(array, axis, pairs)
 
 
+def remote(src, dst, send, recv, axis, index):
+    return pltpu.make_async_remote_copy(
+        src_ref=src, dst_ref=dst, send_sem=send, recv_sem=recv,
+        device_id={axis: index}, device_id_type=pl.DeviceIdType.MESH,
+    )
+
+
+def greet(n, m):
+    i, w = lax.axis_index("lm"), lax.axis_index("kf")
+    barrier = pltpu.get_barrier_semaphore()
+    for k in range(1, n):
+        pl.semaphore_signal(
+            barrier, inc=1, device_id={"lm": lax.rem(i + k, n)}, device_id_type=pl.DeviceIdType.MESH
+        )
+    for k in range(1, m):
+        pl.semaphore_signal(
+            barrier, inc=1, device_id={"kf": lax.rem(w + k, m)}, device_id_type=pl.DeviceIdType.MESH
+        )
+    pl.semaphore_wait(barrier, n - 1 + m - 1)
+
+
+def reduce_spread(n, m, pair, h, full, bufs, sems):
+    fold, acc, rs = bufs
+    fold_s, fold_r, rs_s, rs_r, ag_s, ag_r, fw_s, fw_r = sems
+    own = acc.shape[0]
+    sh = own // n
+    i, w = lax.axis_index("lm"), lax.axis_index("kf")
+    later, former = lax.rem(w + 1, m), lax.rem(w + m - 1, m)
+
+    def at(ref, j, base=0):
+        return ref.at[pl.ds(base + j * sh, sh)]
+
+    order = [lax.rem(i + k, n) for k in range(1, n)] + [i]
+    others = order[:-1]
+    folds = [remote(at(h, j, own), at(fold, j), fold_s.at[k], fold_r.at[k], "kf", later) for k, j in enumerate(order)]
+
+    @pl.when(w < m - 1)
+    def _():
+        for copy in folds:
+            copy.start()
+
+    scatters = [remote(at(acc, j), rs.at[i], rs_s.at[k], rs_r.at[i], "lm", j) for k, j in enumerate(others)]
+    for k, j in enumerate(order):
+        spot = pl.ds(j * sh, sh)
+
+        @pl.when(w > 0)
+        def _():
+            folds[k].wait_recv()
+            acc[spot] = h[spot] + fold[spot]
+
+        @pl.when(w == 0)
+        def _():
+            acc[spot] = h[spot]
+
+        if k < n - 1:
+            scatters[k].start()
+    total = acc[pl.ds(i * sh, sh)]
+    arrive = [lax.rem(i + n - k, n) for k in range(1, n)]
+    for j in arrive:
+        remote(at(acc, j), rs.at[j], rs_s.at[0], rs_r.at[j], "lm", j).wait_recv()
+        total = total + rs[j]
+    full[pl.ds(i * sh, sh)] = total
+    gathers = [remote(at(full, i), at(full, i), ag_s.at[k], ag_r.at[i], "lm", j) for k, j in enumerate(others)]
+    for copy in gathers:
+        copy.start()
+    forwards = []
+    for k, j in enumerate([i] + arrive):
+        if k > 0:
+            remote(at(full, j), at(full, j), ag_s.at[0], ag_r.at[j], "lm", j).wait_recv()
+        if pair:
+            copy = remote(at(full, j), at(full, j, own), fw_s.at[k], fw_r.at[k], "kf", former)
+            forwards.append(copy)
+
+            @pl.when(w > 0)
+            def _():
+                copy.start()
+
+    def finish_pair():
+        @pl.when(w < m - 1)
+        def _():
+            for copy in forwards:
+                copy.wait_recv()
+
+        @pl.when(w == m - 1)
+        def _():
+            full[pl.ds(own, own)] = jnp.zeros((own,) + full.shape[1:], jnp.float32)
+
+    def finish_sends():
+        @pl.when(w < m - 1)
+        def _():
+            for copy in folds:
+                copy.wait_send()
+
+        for copy in scatters + gathers:
+            copy.wait_send()
+        if pair:
+
+            @pl.when(w > 0)
+            def _():
+                for copy in forwards:
+                    copy.wait_send()
+
+    return finish_pair, finish_sends
+
+
+def over_windows(m, value, slots, send, recv):
+    w = lax.axis_index("kf")
+    slots[w] = jnp.sum(value, axis=0)
+    copies = []
+    for k in range(1, m):
+        copy = remote(slots.at[w], slots.at[w], send.at[k], recv.at[w], "kf", lax.rem(w + k, m))
+        copy.start()
+        copies.append(copy)
+    for k in range(1, m):
+        j = lax.rem(w + k, m)
+        remote(slots.at[j], slots.at[j], send.at[0], recv.at[j], "kf", j).wait_recv()
+    total = slots[0]
+    for j in range(1, m):
+        total = total + slots[j]
+
+    def finish():
+        for copy in copies:
+            copy.wait_send()
+
+    return jnp.sum(jnp.sum(total, axis=0, keepdims=True), axis=1, keepdims=True), finish
+
+
+def first_phase(n, m, h, scale, res_out, dir_out, energy_out, full, fold, acc, rs, slots, *sems):
+    own = acc.shape[0]
+    greet(n, m)
+    finish_pair, finish_sends = reduce_spread(n, m, True, h, full, (fold, acc, rs), sems[:8])
+    grad = full[pl.ds(0, own)]
+    energy, finish = over_windows(m, grad * grad * scale[pl.ds(0, own)], slots.at[0], sems[8].at[0], sems[9].at[0])
+    energy_out[...] = jnp.broadcast_to(energy, energy_out.shape)
+    finish_pair()
+    res_out[...] = -full[...]
+    dir_out[...] = -full[...] * scale[...]
+    finish()
+    finish_sends()
+
+
+def middle_phase(n, m, h, res, direction, scale, damp, energy_in, answer_in, res_out, dir_out, energy_out, answer_out, full, fold, acc, rs, slots, *sems):
+    own = acc.shape[0]
+    here = pl.ds(0, own)
+    greet(n, m)
+    finish_pair, finish_sends = reduce_spread(n, m, True, h, full, (fold, acc, rs), sems[:8])
+    energy = energy_in[pl.ds(0, 1), pl.ds(0, 1)]
+    applied = full[here] + damp[here] * direction[here]
+    curve, finish_a = over_windows(m, direction[here] * applied, slots.at[0], sems[8].at[0], sems[9].at[0])
+    step = energy / curve
+    after = res[here] - step * applied
+    fresh, finish_b = over_windows(m, after * after * scale[here], slots.at[1], sems[8].at[1], sems[9].at[1])
+    answer_out[...] = answer_in[...] + step * direction[here]
+    energy_out[...] = jnp.broadcast_to(fresh, energy_out.shape)
+    finish_pair()
+    after = res[...] - step * (full[...] + damp[...] * direction[...])
+    res_out[...] = after
+    dir_out[...] = scale[...] * after + fresh / energy * direction[...]
+    finish_a()
+    finish_b()
+    finish_sends()
+
+
+def last_phase(n, m, h, res, direction, damp, energy_in, answer_in, res_out, answer_out, full, fold, acc, rs, slots, *sems):
+    own = acc.shape[0]
+    here = pl.ds(0, own)
+    greet(n, m)
+    _, finish_sends = reduce_spread(n, m, False, h, full, (fold, acc, rs), sems[:8])
+    applied = full[here] + damp[here] * direction[here]
+    curve, finish = over_windows(m, direction[here] * applied, slots.at[0], sems[8].at[0], sems[9].at[0])
+    step = energy_in[pl.ds(0, 1), pl.ds(0, 1)] / curve
+    answer_out[...] = answer_in[...] + step * direction[here]
+    res_out[...] = res[here] - step * applied
+    finish()
+    finish_sends()
+
+
+def phase(kernel, number, n, m, outs, *operands):
+    pair = operands[0].shape
+    own = pair[0] // 2
+    tile = pair[1:]
+    vmem = pl.BlockSpec(memory_space=pltpu.VMEM)
+    dma = pltpu.SemaphoreType.DMA
+    return pl.pallas_call(
+        functools.partial(kernel, n, m),
+        in_specs=[vmem] * len(operands),
+        out_specs=[vmem] * len(outs),
+        out_shape=[jax.ShapeDtypeStruct(shape, jnp.float32) for shape in outs],
+        scratch_shapes=[
+            pltpu.VMEM(pair, jnp.float32),
+            pltpu.VMEM((own,) + tile, jnp.float32),
+            pltpu.VMEM((own,) + tile, jnp.float32),
+            pltpu.VMEM((n, own // n) + tile, jnp.float32),
+            pltpu.VMEM((2, m) + tile, jnp.float32),
+        ]
+        + [dma((n,))] * 8
+        + [dma((2, m))] * 2,
+        compiler_params=pltpu.CompilerParams(collective_id=number, has_side_effects=True),
+        name=kernel.__name__,
+    )(*operands)
+
+
 def to_groups(array):
     state, frames = array.shape
     padded = jnp.pad(array, ((0, PAD - state), (0, 0)))
@@ -116,33 +318,27 @@
     starts, code = prepare(frame_ids, obs_count, lax.axis_index("kf") * frames, 2 * own)
     jac = jnp.pad(jacobian, ((0, 0), (0, PAD - state), (0, 0)))
     res = residual_rows.astype(jnp.float32)
-    damp, scale = to_groups(damping), to_groups(jacobi_scale)
+    n, m = lax.axis_size("lm"), lax.axis_size("kf")
+    window = jnp.concatenate([to_groups(damping), to_groups(jacobi_scale)], axis=1)
+    window = jnp.concatenate([window, passed_along(window, "kf", -1)], axis=0)
+    damp, scale = window[:, :PAD], window[:, PAD:]
+    pair, one, tile = (2 * own, PAD, LANES), (own, PAD, LANES), (8, LANES)
 
     def product(field):
-        if field is None:
-            pair = jnp.zeros((2 * own, PAD, LANES), jnp.float32)
-        else:
-            pair = jnp.concatenate([field, passed_along(field, "kf", -1)], axis=0)
-        total = local_terms(field is not None, starts, pair, code, res, jac, nullspace)
-        return lax.psum(total[:own] + passed_along(total[own:], "kf", 1), "lm")
-
-    def inner_window(left, right):
-        return lax.psum(jnp.sum(left * right), "kf")
-
-    residual = -product(None)
-    direction = scale * residual
-    energy = inner_window(residual, direction)
-    answer = jnp.zeros_like(residual)
-    for step_index in range(ITERS):
-        applied = product(direction) + damp * direction
-        step_size = energy / inner_window(direction, applied)
-        answer = answer + step_size * direction
-        residual = residual - step_size * applied
-        if step_index + 1 < ITERS:
-            scaled = scale * residual
-            fresh = inner_window(residual, scaled)
-            direction = scaled + fresh / energy * direction
-            energy = fresh
+        used = field is not None
+        held = field if used else jnp.zeros(pair, jnp.float32)
+        return local_terms(used, starts, held, code, res, jac, nullspace)
+
+    residual, direction, energy = phase(first_phase, 0, n, m, (pair, pair, tile), product(None), scale)
+    answer = jnp.zeros(one, jnp.float32)
+    for number in range(1, ITERS):
+        residual, direction, energy, answer = phase(
+            middle_phase, number, n, m, (pair, pair, tile, one),
+            product(direction), residual, direction, scale, damp, energy, answer,
+        )
+    residual, answer = phase(
+        last_phase, ITERS, n, m, (one, one), product(direction), residual, direction, damp, energy, answer
+    )
     return (from_groups(answer, state), from_groups(residual, state))
 
 

time: 418 us -> 202 us (0.48)
  waiting for transfers between devices: 233 us -> 0.01 us
  Pallas kernels: 104 us -> 186 us
  blocking collectives: 19.8 us -> 0 us
  between operations: 17.8 us -> 0.74 us
  starting transfers between devices: 16.7 us -> 1.29 us
  other arithmetic: 16.5 us -> 2.91 us
    psum x3 -> x0, waiting for transfers between devices: 225 us -> none  [product(): return lax.psum(total[:own] + passed_along(total[own:], 'kf', 1), 'lm')]
    pallas_call x0 -> x3, Pallas kernels: none -> 81.9 us  [phase(): pl.pallas_call(functools.partial(kernel, n, m), in_specs=[vmem] * len(ope...]
    psum x3 -> x0, blocking collectives: 19.8 us -> none  [inner_window(): return lax.psum(jnp.sum(left * right), 'kf')]
    ppermute x5 -> x1, starting transfers between devices: 16.6 us -> 1.29 us  [passed_along(): return lax.ppermute(array, axis, pairs)]
    ppermute x5 -> x1, waiting for transfers between devices: 7.64 us -> 0.01 us  [passed_along(): return lax.ppermute(array, axis, pairs)]
    add x4 -> x0, other arithmetic: 5.1 us -> none  [the longest x3 5.05 us: product(): return lax.psum(total[:own] + passed_along(total[own:], 'kf', 1), 'lm')]
    reduce_sum x3 -> x0, other arithmetic: 4.91 us -> none  [inner_window(): return lax.psum(jnp.sum(left * right), 'kf')]
  transfers between devices with their start and end apart: 8 -> 1, of which waited for: 8 -> 0; matrix products, arithmetic and copies ran while one was open for 0% -> 3% of each run, Pallas kernels for 0% -> 12%
where the time goes in v2:
time: 202 us
  Pallas kernels  186 us (92%)
  local copies, waits for them, and re-layouts  9.74 us (5%)
  other arithmetic  2.91 us (1%)
    pallas_call x3, Pallas kernels, local_terms(): pl.pallas_call(functools.partial(local_kernel, use_field), grid_spec=pltp...  104 us
    pallas_call x3, Pallas kernels, phase(): pl.pallas_call(functools.partial(kernel, n, m), in_specs=[vmem] * len(ope...  81.9 us
  transfers between devices with their start and end apart: 1, of which 0 were waited for; matrix products, arithmetic and copies ran while one was open for 3% of the time, Pallas kernels for 12%

profile of v2, /device:TPU:0, one launch (start us, length us, event | category | flops | bytes accessed | tf_op | source)
XLA Modules:
  0.0 201.7 jit_solution(14682154410595426302)
XLA Ops:
  0.6 1.1 bitcast_bitcast_fusion
  1.7 0.1 pad_maximum_fusion.1
  1.8 1.3 collective-permute-start
  3.1 0.8 broadcast_subtract_fusion
  3.9 0.6 fusion.10.starts
  4.5 1.4 convert_element_type.17.res_ref
  5.8 1.4 copy.10
  7.2 0.9 pad.11.jac_ref
  8.1 0.9 fusion.code_ref
  9.0 0.8 broadcast_in_dim.12.field_ref
  9.8 24.3 %local_gradient.1.h = f32[64,16,128]{2,1,0:T(8,128)} custom-call(s32[128]{0:T(128)} %fusion.10.starts, f32[64,16,128]{2,1,0:T(8,128)} %broadcast_in_dim.12.field_ref, s32[128,128]{1,0:T(8,128)} %fusion.code_ref, f32[128,128]{1,0:T(8,128)} %convert_element_type.17.res_ref, bf16[128,16,128]{2,1,0:T(8,128)(2,1)} %pad.11.jac_ref, bf16[128,128,128]{2,1,0:T(8,128)(2,1)} %null_ref.5), custom_call_target="tpu_custom_call" | custom-call | tf_op jit(solution)/shard_map/local_gradient/pallas_call | solution.py:65
  34.1 0.0 collective-permute-done
  34.1 0.1 pad_maximum_fusion
  34.2 1.1 fusion.12
  35.3 29.6 %first_phase.1 = (f32[64,16,128]{2,1,0:T(8,128)}, f32[64,16,128]{2,1,0:T(8,128)}, f32[8,128]{1,0:T(8,128)}) custom-call(f32[64,16,128]{2,1,0:T(8,128)} %local_gradient.1.h, f32[64,16,128]{2,1,0:T(8,128)} %get-tuple-element.21.scale), custom_call_target="tpu_custom_call" | custom-call | tf_op jit(solution)/shard_map/first_phase/pallas_call | solution.py:273
  64.9 40.0 %local_field.2.h = f32[64,16,128]{2,1,0:T(8,128)} custom-call(s32[128]{0:T(128)} %fusion.10.starts, f32[64,16,128]{2,1,0:T(8,128)} %get-tuple-element.11.field_ref.direction, s32[128,128]{1,0:T(8,128)} %fusion.code_ref, f32[128,128]{1,0:T(8,128)} %convert_element_type.17.res_ref, bf16[128,16,128]{2,1,0:T(8,128)(2,1)} %pad.11.jac_ref, ...), custom_call_target="tpu_custom_call" | custom-call | tf_op jit(solution)/shard_map/local_field/pallas_call | solution.py:65
  104.8 0.7 broadcast_in_dim.14.answer_in
  105.6 27.3 %middle_phase.1 = (f32[64,16,128]{2,1,0:T(8,128)}, f32[64,16,128]{2,1,0:T(8,128)}, f32[8,128]{1,0:T(8,128)}, f32[32,16,128]{2,1,0:T(8,128)}) custom-call(f32[64,16,128]{2,1,0:T(8,128)} %local_field.2.h, f32[64,16,128]{2,1,0:T(8,128)} %get-tuple-element.12.res, f32[64,16,128]{2,1,0:T(8,128)} %get-tuple-element.11.field_ref.direction, ...), custom_call_target="tpu_custom_call" | custom-call | tf_op jit(solution)/shard_map/middle_phase/pallas_call | solution.py:273
  132.9 40.0 %local_field.3.h = f32[64,16,128]{2,1,0:T(8,128)} custom-call(s32[128]{0:T(128)} %fusion.10.starts, f32[64,16,128]{2,1,0:T(8,128)} %get-tuple-element.14.field_ref.direction, s32[128,128]{1,0:T(8,128)} %fusion.code_ref, f32[128,128]{1,0:T(8,128)} %convert_element_type.17.res_ref, bf16[128,16,128]{2,1,0:T(8,128)(2,1)} %pad.11.jac_ref, ...), custom_call_target="tpu_custom_call" | custom-call | tf_op jit(solution)/shard_map/local_field/pallas_call | solution.py:65
  172.8 25.0 %last_phase.1 = (f32[32,16,128]{2,1,0:T(8,128)}, f32[32,16,128]{2,1,0:T(8,128)}) custom-call(f32[64,16,128]{2,1,0:T(8,128)} %local_field.3.h, f32[64,16,128]{2,1,0:T(8,128)} %get-tuple-element.15.res, f32[64,16,128]{2,1,0:T(8,128)} %get-tuple-element.14.field_ref.direction, f32[64,16,128]{2,1,0:T(8,128)} %get-tuple-element.20.damp, ...), custom_call_target="tpu_custom_call" | custom-call | tf_op jit(solution)/shard_map/last_phase/pallas_call | solution.py:273
  197.8 1.0 copy.13
  198.9 1.0 copy.14
  199.9 0.9 copy.18
  200.8 0.9 copy.17
  (7 shorter events, 0.1 us)
Async XLA Ops:
  0.6 7.5 %copy-start = (s32[128]{0:T(128)S(1)}, s32[128]{0:T(128)}, u32[]{:S(2)}) copy-start(s32[128]{0:T(128)} %param.11) | copy-start | bytes 1540
  1.8 32.3 %collective-permute-start = (f32[32,32,128]{2,1,0:T(8,128)S(1)}, f32[32,32,128]{2,1,0:T(8,128)S(1)}, u32[]{:S(2)}, u32[]{:S(2)}) collective-permute-start(f32[32,32,128]{2,1,0:T(8,128)S(1)} %pad_maximum_fusion.1), channel_id=1, source_target_pairs={{1,0},{2,1},{3,2},{5,4},{6,5},{7,6},{9,8},{10,9},{11,10},{13,12},{... | collective-permute-start | bytes 1572872 | tf_op jit(solution)/shard_map/ppermute | solution.py:87

commit v3 on v2

--- a/solution.py
+++ b/solution.py
@@ -14,7 +14,7 @@
 CHUNK = 16
 
 
-def local_kernel(use_field, starts, field_ref, code_ref, res_ref, jac_ref, null_ref, out_ref):
+def local_kernel(use_field, starts, field_ref, code_ref, res_ref, jac_ref, null_ref, out_ref, hot_ref, row_ref):
     step = pl.program_id(0)
 
     @pl.when(step == 0)
@@ -22,41 +22,43 @@
         out_ref[...] = jnp.zeros_like(out_ref)
 
     lane_iota = lax.broadcasted_iota(jnp.int32, (LANES, LANES), 0)
-
-    def one(i):
-        start = starts[step * CHUNK + i]
-        code = code_ref[pl.ds(i, 1), :]
-        part = code >> 7
-        hot = jnp.where(lane_iota == (code & (LANES - 1)), 1.0, 0.0).astype(jnp.bfloat16)
-        jac = jac_ref[i].astype(jnp.float32)
-        null = null_ref[i]
-        if use_field:
-            window = field_ref[pl.ds(start, SPAN)].reshape(SPAN * PAD, LANES).astype(jnp.bfloat16)
-            spots = jnp.dot(window, hot, preferred_element_type=jnp.float32)
+    codes = [code_ref[pl.ds(i, 1), :] for i in range(CHUNK)]
+    begin = [starts[step * CHUNK + i] for i in range(CHUNK)]
+    for i in range(CHUNK):
+        hot = lane_iota == (codes[i] & (LANES - 1))
+        hot_ref[i] = jnp.where(hot, 1.0, 0.0).astype(jnp.bfloat16)
+    if use_field:
+        for i in range(CHUNK):
+            window = field_ref[pl.ds(begin[i], SPAN)].reshape(SPAN * PAD, LANES).astype(jnp.bfloat16)
+            spots = jnp.dot(window, hot_ref[i], preferred_element_type=jnp.float32)
+            part = codes[i] >> 7
             gathered = jnp.zeros((PAD, LANES), jnp.float32)
             for q in range(SPAN):
                 gathered = jnp.where(part == q, spots[q * PAD:(q + 1) * PAD], gathered)
-            lifted = jnp.sum(jac * gathered, axis=0, keepdims=True)
-        else:
-            lifted = jnp.where(code >= 0, res_ref[pl.ds(i, 1), :], 0.0)
-        inner = jnp.dot(
-            lifted.astype(jnp.bfloat16), null, preferred_element_type=jnp.float32
-        ).astype(jnp.bfloat16)
-        spread = lax.dot_general(
-            inner, null, (((1,), (1,)), ((), ())), preferred_element_type=jnp.float32
+            jac = jac_ref[i].astype(jnp.float32)
+            row_ref[pl.ds(i, 1), :] = jnp.sum(jac * gathered, axis=0, keepdims=True)
+    else:
+        row_ref[...] = jnp.where(code_ref[...] >= 0, res_ref[...], 0.0)
+    inner = []
+    for i in range(CHUNK):
+        lifted = row_ref[pl.ds(i, 1), :].astype(jnp.bfloat16)
+        inner.append(jnp.dot(lifted, null_ref[i], preferred_element_type=jnp.float32).astype(jnp.bfloat16))
+    for i in range(CHUNK):
+        row_ref[pl.ds(i, 1), :] = lax.dot_general(
+            inner[i], null_ref[i], (((1,), (1,)), ((), ())), preferred_element_type=jnp.float32
         )
-        terms = jac * spread
+    back = []
+    for i in range(CHUNK):
+        part = codes[i] >> 7
+        terms = jac_ref[i].astype(jnp.float32) * row_ref[pl.ds(i, 1), :]
         placed = jnp.concatenate(
             [jnp.where(part == q, terms, 0.0) for q in range(SPAN)], axis=0
         ).astype(jnp.bfloat16)
-        back = lax.dot_general(
-            placed, hot, (((1,), (1,)), ((), ())), preferred_element_type=jnp.float32
-        )
-        return start, back.reshape(SPAN, PAD, LANES)
-
-    for i in range(CHUNK):
-        start, back = one(i)
-        out_ref[pl.ds(start, SPAN)] += back
+        back.append(lax.dot_general(
+            placed, hot_ref[i], (((1,), (1,)), ((), ())), preferred_element_type=jnp.float32
+        ).reshape(SPAN, PAD, LANES))
+    for i in range(CHUNK):
+        out_ref[pl.ds(begin[i], SPAN)] += back[i]
 
 
 def local_terms(use_field, starts, field, code, res, jac, null):
@@ -75,6 +77,10 @@
                 pl.BlockSpec((CHUNK, LANES, LANES), lambda b, s: (b, 0, 0)),
             ],
             out_specs=pl.BlockSpec((groups, PAD, LANES), lambda b, s: (0, 0, 0)),
+            scratch_shapes=[
+                pltpu.VMEM((CHUNK, LANES, LANES), jnp.bfloat16),
+                pltpu.VMEM((CHUNK, LANES), jnp.float32),
+            ],
         ),
         out_shape=jax.ShapeDtypeStruct((groups, PAD, LANES), jnp.float32),
         name="local_field" if use_field else "local_gradient",

time: 202 us -> 133 us (0.66)
  Pallas kernels: 186 us -> 117 us
    pallas_call x3, Pallas kernels: 104 us -> 34.7 us  [local_terms(): pl.pallas_call(functools.partial(local_kernel, use_field), grid_spec=pltp...]
  transfers between devices with their start and end apart: 1 -> 1, of which waited for: 0 -> 0; matrix products, arithmetic and copies ran while one was open for 3% -> 5% of each run, Pallas kernels for 12% -> 8%
where the time goes in v3:
time: 133 us; the launch traced here: 132 us
  Pallas kernels  117 us (88%)
  local copies, waits for them, and re-layouts  9.74 us (7%)
  other arithmetic  2.91 us (2%)
    pallas_call x3, Pallas kernels, phase(): pl.pallas_call(functools.partial(kernel, n, m), in_specs=[vmem] * len(ope...  81.9 us
    pallas_call x3, Pallas kernels, local_terms(): pl.pallas_call(functools.partial(local_kernel, use_field), grid_spec=pltp...  34.7 us
    unnamed x7, local copies, waits for them, and re-layouts  3.11 us
  transfers between devices with their start and end apart: 1, of which 0 were waited for; matrix products, arithmetic and copies ran while one was open for 5% of the time, Pallas kernels for 8%

profile of v3, /device:TPU:0, one launch (start us, length us, event | category | flops | bytes accessed | tf_op | source)
XLA Modules:
  0.0 132.2 jit_solution(5597247488127819401)
XLA Ops:
  0.6 1.1 bitcast_bitcast_fusion
  1.7 0.1 pad_maximum_fusion.1
  1.8 1.3 collective-permute-start
  3.1 0.8 broadcast_subtract_fusion
  3.9 0.6 fusion.10.starts
  4.5 1.4 %convert_element_type.17.res_ref = f32[128,128]{1,0:T(8,128)} convert(bf16[128,128]{1,0:T(8,128)(2,1)} %param.7) | non-fusion elementwise | flops 16384 | bytes 98304 | tf_op jit(solution)/shard_map/convert_element_type | solution.py:326
  5.8 1.4 %copy.10 = bf16[128,15,128]{2,1,0:T(8,128)(2,1)S(1)} copy(bf16[128,15,128]{2,0,1:T(8,128)(2,1)} %param.8) | data formatting | bytes 983040 | tf_op args[1]
  7.2 0.9 pad.11.jac_ref
  8.1 0.9 fusion.code_ref
  9.0 0.8 broadcast_in_dim.12.field_ref
  9.8 10.8 %local_gradient.1.h = f32[64,16,128]{2,1,0:T(8,128)} custom-call(s32[128]{0:T(128)} %fusion.10.starts, f32[64,16,128]{2,1,0:T(8,128)} %broadcast_in_dim.12.field_ref, s32[128,128]{1,0:T(8,128)} %fusion.code_ref, f32[128,128]{1,0:T(8,128)} %convert_element_type.17.res_ref, bf16[128,16,128]{2,1,0:T(8,128)(2,1)} %pad.11.jac_ref, bf16[128,128,128]{2,1,0:T(8,128)(2,1)} %null_ref.5), custom_call_target="tpu_custom_call" | custom-call | tf_op jit(solution)/shard_map/local_gradient/pallas_call | solution.py:67
  20.6 0.0 collective-permute-done
  20.6 0.1 pad_maximum_fusion
  20.7 1.1 fusion.12
  21.8 29.6 %first_phase.1 = (f32[64,16,128]{2,1,0:T(8,128)}, f32[64,16,128]{2,1,0:T(8,128)}, f32[8,128]{1,0:T(8,128)}) custom-call(f32[64,16,128]{2,1,0:T(8,128)} %local_gradient.1.h, f32[64,16,128]{2,1,0:T(8,128)} %get-tuple-element.21.scale), custom_call_target="tpu_custom_call" | custom-call | tf_op jit(solution)/shard_map/first_phase/pallas_call | solution.py:279
  51.4 12.0 %local_field.2.h = f32[64,16,128]{2,1,0:T(8,128)} custom-call(s32[128]{0:T(128)} %fusion.10.starts, f32[64,16,128]{2,1,0:T(8,128)} %get-tuple-element.11.field_ref.direction, s32[128,128]{1,0:T(8,128)} %fusion.code_ref, f32[128,128]{1,0:T(8,128)} %convert_element_type.17.res_ref, bf16[128,16,128]{2,1,0:T(8,128)(2,1)} %pad.11.jac_ref, ...), custom_call_target="tpu_custom_call" | custom-call | tf_op jit(solution)/shard_map/local_field/pallas_call | solution.py:67
  63.3 0.7 broadcast_in_dim.14.answer_in
  64.1 27.3 %middle_phase.1 = (f32[64,16,128]{2,1,0:T(8,128)}, f32[64,16,128]{2,1,0:T(8,128)}, f32[8,128]{1,0:T(8,128)}, f32[32,16,128]{2,1,0:T(8,128)}) custom-call(f32[64,16,128]{2,1,0:T(8,128)} %local_field.2.h, f32[64,16,128]{2,1,0:T(8,128)} %get-tuple-element.12.res, f32[64,16,128]{2,1,0:T(8,128)} %get-tuple-element.11.field_ref.direction, ...), custom_call_target="tpu_custom_call" | custom-call | tf_op jit(solution)/shard_map/middle_phase/pallas_call | solution.py:279
  91.4 12.0 %local_field.3.h = f32[64,16,128]{2,1,0:T(8,128)} custom-call(s32[128]{0:T(128)} %fusion.10.starts, f32[64,16,128]{2,1,0:T(8,128)} %get-tuple-element.14.field_ref.direction, s32[128,128]{1,0:T(8,128)} %fusion.code_ref, f32[128,128]{1,0:T(8,128)} %convert_element_type.17.res_ref, bf16[128,16,128]{2,1,0:T(8,128)(2,1)} %pad.11.jac_ref, ...), custom_call_target="tpu_custom_call" | custom-call | tf_op jit(solution)/shard_map/local_field/pallas_call | solution.py:67
  103.4 25.0 %last_phase.1 = (f32[32,16,128]{2,1,0:T(8,128)}, f32[32,16,128]{2,1,0:T(8,128)}) custom-call(f32[64,16,128]{2,1,0:T(8,128)} %local_field.3.h, f32[64,16,128]{2,1,0:T(8,128)} %get-tuple-element.15.res, f32[64,16,128]{2,1,0:T(8,128)} %get-tuple-element.14.field_ref.direction, f32[64,16,128]{2,1,0:T(8,128)} %get-tuple-element.20.damp, ...), custom_call_target="tpu_custom_call" | custom-call | tf_op jit(solution)/shard_map/last_phase/pallas_call | solution.py:279
  128.4 1.0 copy.13
  129.4 1.0 copy.14
  130.5 0.9 copy.18
  131.3 0.9 copy.17
  (7 shorter events, 0.1 us)
Async XLA Ops:
  0.6 7.5 %copy-start = (s32[128]{0:T(128)S(1)}, s32[128]{0:T(128)}, u32[]{:S(2)}) copy-start(s32[128]{0:T(128)} %param.11) | copy-start | bytes 1540
  1.8 18.8 %collective-permute-start = (f32[32,32,128]{2,1,0:T(8,128)S(1)}, f32[32,32,128]{2,1,0:T(8,128)S(1)}, u32[]{:S(2)}, u32[]{:S(2)}) collective-permute-start(f32[32,32,128]{2,1,0:T(8,128)S(1)} %pad_maximum_fusion.1), channel_id=1, source_target_pairs={{1,0},{2,1},{3,2},{5,4},{6,5},{7,6},{9,8},{10,9},{11,10},{13,12},{... | collective-permute-start | bytes 1572872 | tf_op jit(solution)/shard_map/ppermute | solution.py:93

commit v4 on v3

v4 whole, which is shorter than its diff:
```python
import functools

import jax
import jax.numpy as jnp
from jax import lax
from jax.experimental import pallas as pl
from jax.experimental.pallas import tpu as pltpu
from jax.sharding import PartitionSpec as P

ITERS = 2
LANES = 128
PAD = 16
SPAN = 5
CHUNK = 16


def local_kernel(use_field, starts, field_ref, code_ref, jac_ref, null_ref, out_ref, hot_ref, row_ref):
    step = pl.program_id(0)

    @pl.when(step == 0)
    def _():
        out_ref[...] = jnp.zeros_like(out_ref)

    lane_iota = lax.broadcasted_iota(jnp.int32, (LANES, LANES), 0)
    codes = [code_ref[pl.ds(i, 1), :] for i in range(CHUNK)]
    begin = [starts[step * CHUNK + i] for i in range(CHUNK)]
    for i in range(CHUNK):
        hot = lane_iota == (codes[i] & (LANES - 1))
        hot_ref[i] = jnp.where(hot, 1.0, 0.0).astype(jnp.bfloat16)
    if use_field:
        for i in range(CHUNK):
            window = field_ref[pl.ds(begin[i], SPAN)].reshape(SPAN * PAD, LANES).astype(jnp.bfloat16)
            spots = jnp.dot(window, hot_ref[i], preferred_element_type=jnp.float32)
            part = codes[i] >> 7
            gathered = jnp.zeros((PAD, LANES), jnp.float32)
            for q in range(SPAN):
                gathered = jnp.where(part == q, spots[q * PAD:(q + 1) * PAD], gathered)
            jac = jac_ref[i].astype(jnp.float32)
            row_ref[pl.ds(i, 1), :] = jnp.sum(jac * gathered, axis=0, keepdims=True)
    else:
        row_ref[...] = jnp.where(code_ref[...] >= 0, field_ref[...].astype(jnp.float32), 0.0)
    inner = []
    for i in range(CHUNK):
        lifted = row_ref[pl.ds(i, 1), :].astype(jnp.bfloat16)
        inner.append(jnp.dot(lifted, null_ref[i], preferred_element_type=jnp.float32).astype(jnp.bfloat16))
    for i in range(CHUNK):
        row_ref[pl.ds(i, 1), :] = lax.dot_general(
            inner[i], null_ref[i], (((1,), (1,)), ((), ())), preferred_element_type=jnp.float32
        )
    back = []
    for i in range(CHUNK):
        part = codes[i] >> 7
        terms = jac_ref[i].astype(jnp.float32) * row_ref[pl.ds(i, 1), :]
        placed = jnp.concatenate(
            [jnp.where(part == q, terms, 0.0) for q in range(SPAN)], axis=0
        ).astype(jnp.bfloat16)
        back.append(lax.dot_general(
            placed, hot_ref[i], (((1,), (1,)), ((), ())), preferred_element_type=jnp.float32
        ).reshape(SPAN, PAD, LANES))
    for i in range(CHUNK):
        out_ref[pl.ds(begin[i], SPAN)] += back[i]


def local_terms(use_field, starts, field, code, jac, null, groups):
    blocks = null.shape[0]
    if use_field:
        source = pl.BlockSpec(field.shape, lambda b, s: (0, 0, 0))
    else:
        source = pl.BlockSpec((CHUNK, LANES), lambda b, s: (b, 0))
    return pl.pallas_call(
        functools.partial(local_kernel, use_field),
        grid_spec=pltpu.PrefetchScalarGridSpec(
            num_scalar_prefetch=1,
            grid=(blocks // CHUNK,),
            in_specs=[
                source,
                pl.BlockSpec((CHUNK, LANES), lambda b, s: (b, 0)),
                pl.BlockSpec((CHUNK, PAD, LANES), lambda b, s: (b, 0, 0)),
                pl.BlockSpec((CHUNK, LANES, LANES), lambda b, s: (b, 0, 0)),
            ],
            out_specs=pl.BlockSpec((groups, PAD, LANES), lambda b, s: (0, 0, 0)),
            scratch_shapes=[
                pltpu.VMEM((CHUNK, LANES, LANES), jnp.bfloat16),
                pltpu.VMEM((CHUNK, LANES), jnp.float32),
            ],
        ),
        out_shape=jax.ShapeDtypeStruct((groups, PAD, LANES), jnp.float32),
        name="local_field" if use_field else "local_gradient",
    )(starts, field, code, jac, null)


def remote(src, dst, send, recv, axis, index):
    return pltpu.make_async_remote_copy(
        src_ref=src, dst_ref=dst, send_sem=send, recv_sem=recv,
        device_id={axis: index}, device_id_type=pl.DeviceIdType.MESH,
    )


def greet(n, m):
    i, w = lax.axis_index("lm"), lax.axis_index("kf")
    barrier = pltpu.get_barrier_semaphore()
    peers = [("lm", i + 1 - 2 * lax.rem(i, 2))]
    peers += [("lm", lax.rem(i + 2 * k, n)) for k in range(1, n // 2)]
    peers += [("kf", lax.rem(w + k, m)) for k in range(1, m)]
    for axis, index in peers:
        pl.semaphore_signal(barrier, inc=1, device_id={axis: index}, device_id_type=pl.DeviceIdType.MESH)
    pl.semaphore_wait(barrier, len(peers))


def reduce_spread(n, m, pair, h, full, bufs, sems):
    fold, acc, twin, rs = bufs
    fold_s, fold_r, tw_s, tw_r, rs_s, rs_r, ag_s, xs_s, ag_r, fw_s, fw_r = sems
    own = acc.shape[0]
    sh = own // n
    hi = n // 2
    i, w = lax.axis_index("lm"), lax.axis_index("kf")
    z, x = i // 2, lax.rem(i, 2)
    partner = i + 1 - 2 * x
    later, former = lax.rem(w + 1, m), lax.rem(w + m - 1, m)

    def at(ref, j, base=0):
        return ref.at[pl.ds(base + j * sh, sh)]

    levels = [lax.rem(z + k, hi) for k in range(1, hi)] + [z]
    near = [2 * level + x for level in levels]
    far = [2 * level + 1 - x for level in levels]
    order = [j for k in range(hi) for j in (far[k], near[k])]
    folds = [remote(at(h, j, own), at(fold, j), fold_s.at[k], fold_r.at[k], "kf", later) for k, j in enumerate(order)]

    @pl.when(w < m - 1)
    def _():
        for copy in folds:
            copy.start()

    twins = [remote(at(acc, far[k]), twin.at[k], tw_s.at[k], tw_r.at[k], "lm", partner) for k in range(hi)]
    scatters = [remote(at(acc, near[k]), rs.at[z], rs_s.at[k], rs_r.at[z], "lm", near[k]) for k in range(hi - 1)]

    def take(k):
        spot = pl.ds(order[k] * sh, sh)

        @pl.when(w > 0)
        def _():
            folds[k].wait_recv()
            acc[spot] = h[spot] + fold[spot]

        @pl.when(w == 0)
        def _():
            acc[spot] = h[spot]

    def join(k):
        twins[k].wait_recv()
        spot = pl.ds(near[k] * sh, sh)
        acc[spot] = acc[spot] + twin[k]
        if k < hi - 1:
            scatters[k].start()

    for k in range(hi):
        take(2 * k)
        twins[k].start()
        take(2 * k + 1)
        if k > 0:
            join(k - 1)
    join(hi - 1)
    total = acc[pl.ds(i * sh, sh)]
    arrive = [lax.rem(z + hi - k, hi) for k in range(1, hi)]
    for level in arrive:
        j = 2 * level + x
        remote(at(acc, j), rs.at[level], rs_s.at[0], rs_r.at[level], "lm", j).wait_recv()
        total = total + rs[level]
    full[pl.ds(i * sh, sh)] = total
    gathers = [remote(at(full, i), at(full, i), ag_s.at[k], ag_r.at[i], "lm", near[k]) for k in range(hi - 1)]
    for copy in gathers:
        copy.start()
    crosses, forwards = [], []

    def pass_on(j, cross):
        if cross:
            copy = remote(at(full, j), at(full, j), xs_s.at[len(crosses)], ag_r.at[j], "lm", partner)
            copy.start()
            crosses.append(copy)
        if pair:
            ahead = remote(at(full, j), at(full, j, own), fw_s.at[len(forwards)], fw_r.at[len(forwards)], "kf", former)
            forwards.append(ahead)

            @pl.when(w > 0)
            def _():
                ahead.start()

    def landed(j):
        remote(at(full, j), at(full, j), ag_s.at[0], ag_r.at[j], "lm", partner).wait_recv()

    held = [z] + arrive
    pass_on(i, True)
    for k in range(1, hi + 1):
        if k < hi:
            landed(2 * held[k] + x)
            pass_on(2 * held[k] + x, True)
        landed(2 * held[k - 1] + 1 - x)
        pass_on(2 * held[k - 1] + 1 - x, False)

    def finish_pair():
        @pl.when(w < m - 1)
        def _():
            for copy in forwards:
                copy.wait_recv()

        @pl.when(w == m - 1)
        def _():
            full[pl.ds(own, own)] = jnp.zeros((own,) + full.shape[1:], jnp.float32)

    def finish_sends():
        @pl.when(w < m - 1)
        def _():
            for copy in folds:
                copy.wait_send()

        for copy in twins + scatters + gathers + crosses:
            copy.wait_send()
        if pair:

            @pl.when(w > 0)
            def _():
                for copy in forwards:
                    copy.wait_send()

    return finish_pair, finish_sends


def over_windows(m, value, slots, send, recv):
    w = lax.axis_index("kf")
    slots[w] = jnp.sum(value, axis=0)
    copies = []
    for k in range(1, m):
        copy = remote(slots.at[w], slots.at[w], send.at[k], recv.at[w], "kf", lax.rem(w + k, m))
        copy.start()
        copies.append(copy)
    for k in range(1, m):
        j = lax.rem(w + k, m)
        remote(slots.at[j], slots.at[j], send.at[0], recv.at[j], "kf", j).wait_recv()
    total = slots[0]
    for j in range(1, m):
        total = total + slots[j]

    def finish():
        for copy in copies:
            copy.wait_send()

    return jnp.sum(jnp.sum(total, axis=0, keepdims=True), axis=1, keepdims=True), finish


def columns(g):
    return pl.ds(g * LANES, LANES)


def first_phase(n, m, h, damping, jacobi_scale, res_out, dir_out, energy_out, diag_out, full, fold, acc, twin, rs, slots, diag, *sems):
    own = acc.shape[0]
    state = damping.shape[0]
    w = lax.axis_index("kf")
    diag[...] = jnp.zeros_like(diag)
    for g in range(own):
        diag[g, pl.ds(0, state), :] = damping[:, columns(g)]
        diag[g, pl.ds(PAD, state), :] = jacobi_scale[:, columns(g)]
    greet(n, m)
    diag_copy = remote(
        diag.at[pl.ds(0, own)], diag.at[pl.ds(own, own)], sems[13].at[0], sems[13].at[1], "kf", lax.rem(w + m - 1, m)
    )

    @pl.when(w > 0)
    def _():
        diag_copy.start()

    finish_pair, finish_sends = reduce_spread(n, m, True, h, full, (fold, acc, twin, rs), sems[:11])
    grad = full[pl.ds(0, own)]
    scale = diag[pl.ds(0, own), pl.ds(PAD, PAD), :]
    energy, finish = over_windows(m, grad * grad * scale, slots.at[0], sems[11].at[0], sems[12].at[0])
    energy_out[...] = jnp.broadcast_to(energy, energy_out.shape)
    finish_pair()

    @pl.when(w < m - 1)
    def _():
        diag_copy.wait_recv()

    @pl.when(w > 0)
    def _():
        diag_copy.wait_send()

    res_out[...] = -full[...]
    dir_out[...] = -full[...] * diag[:, pl.ds(PAD, PAD), :]
    diag_out[...] = diag[...]
    finish()
    finish_sends()


def middle_phase(begun, n, m, h, res, direction, diag, energy_in, *rest):
    if begun:
        answer_in, *rest = rest
    res_out, dir_out, energy_out, answer_out, full, fold, acc, twin, rs, slots, *sems = rest
    own = acc.shape[0]
    here, damp, scale = pl.ds(0, own), pl.ds(0, PAD), pl.ds(PAD, PAD)
    greet(n, m)
    finish_pair, finish_sends = reduce_spread(n, m, True, h, full, (fold, acc, twin, rs), sems[:11])
    energy = energy_in[pl.ds(0, 1), pl.ds(0, 1)]
    applied = full[here] + diag[here, damp, :] * direction[here]
    curve, finish_a = over_windows(m, direction[here] * applied, slots.at[0], sems[11].at[0], sems[12].at[0])
    step = energy / curve
    after = res[here] - step * applied
    fresh, finish_b = over_windows(m, after * after * diag[here, scale, :], slots.at[1], sems[11].at[1], sems[12].at[1])
    gained = step * direction[here]
    answer_out[...] = answer_in[...] + gained if begun else gained
    energy_out[...] = jnp.broadcast_to(fresh, energy_out.shape)
    finish_pair()
    after = res[...] - step * (full[...] + diag[:, damp, :] * direction[...])
    res_out[...] = after
    dir_out[...] = diag[:, scale, :] * after + fresh / energy * direction[...]
    finish_a()
    finish_b()
    finish_sends()


def last_phase(n, m, h, res, direction, diag, energy_in, answer_in, res_out, answer_out, full, fold, acc, twin, rs, slots, *sems):
    own = acc.shape[0]
    state = res_out.shape[0]
    here = pl.ds(0, own)
    greet(n, m)
    _, finish_sends = reduce_spread(n, m, False, h, full, (fold, acc, twin, rs), sems[:11])
    applied = full[here] + diag[here, pl.ds(0, PAD), :] * direction[here]
    curve, finish = over_windows(m, direction[here] * applied, slots.at[0], sems[11].at[0], sems[12].at[0])
    step = energy_in[pl.ds(0, 1), pl.ds(0, 1)] / curve
    for g in range(own):
        answer_out[:, columns(g)] = (answer_in[g] + step * direction[g])[:state]
        res_out[:, columns(g)] = (res[g] - step * (full[g] + diag[g, pl.ds(0, PAD), :] * direction[g]))[:state]
    finish()
    finish_sends()


def phase(kernel, name, number, n, m, outs, extra, *operands):
    pair = operands[0].shape
    own = pair[0] // 2
    tile = pair[1:]
    vmem = pl.BlockSpec(memory_space=pltpu.VMEM)
    dma = pltpu.SemaphoreType.DMA
    return pl.pallas_call(
        functools.partial(kernel, n, m),
        in_specs=[vmem] * len(operands),
        out_specs=[vmem] * len(outs),
        out_shape=[jax.ShapeDtypeStruct(shape, jnp.float32) for shape in outs],
        scratch_shapes=[
            pltpu.VMEM(pair, jnp.float32),
            pltpu.VMEM((own,) + tile, jnp.float32),
            pltpu.VMEM((own,) + tile, jnp.float32),
            pltpu.VMEM((n // 2, own // n) + tile, jnp.float32),
            pltpu.VMEM((n // 2, own // n) + tile, jnp.float32),
            pltpu.VMEM((2, m) + tile, jnp.float32),
        ]
        + [pltpu.VMEM(shape, jnp.float32) for shape in extra]
        + [dma((n,))] * 11
        + [dma((2, m))] * 2
        + [dma((2,))],
        compiler_params=pltpu.CompilerParams(collective_id=number, has_side_effects=True),
        name=name,
    )(*operands)


def prepare(frame_ids, obs_count, first_frame, groups):
    rel = frame_ids - first_frame
    starts = jnp.minimum(rel[:, 0] // LANES, groups - SPAN)
    slots = lax.broadcasted_iota(jnp.int32, rel.shape, 1)
    off = jnp.where(slots < obs_count[:, None], rel - starts[:, None] * LANES, -1)
    twice = (
        lax.broadcasted_iota(jnp.int32, (rel.shape[1], 2 * rel.shape[1]), 0)
        == lax.broadcasted_iota(jnp.int32, (rel.shape[1], 2 * rel.shape[1]), 1) // 2
    ).astype(jnp.float32)
    code = jnp.dot(off.astype(jnp.float32), twice, precision=lax.Precision.HIGHEST)
    return starts, jnp.round(code).astype(jnp.int32)


def shards(residual_rows, jacobian, nullspace, frame_ids, obs_count, damping, jacobi_scale):
    state, frames = damping.shape
    own = frames // LANES
    starts, code = prepare(frame_ids, obs_count, lax.axis_index("kf") * frames, 2 * own)
    jac = jnp.pad(jacobian, ((0, 0), (0, PAD - state), (0, 0)))
    n, m = lax.axis_size("lm"), lax.axis_size("kf")
    pair, one, tile = (2 * own, PAD, LANES), (own, PAD, LANES), (8, LANES)
    both = (2 * own, 2 * PAD, LANES)

    def product(field):
        return local_terms(True, starts, field, code, jac, nullspace, 2 * own)

    gradient = local_terms(False, starts, residual_rows, code, jac, nullspace, 2 * own)
    residual, direction, energy, diag = phase(
        first_phase, "first_phase", 0, n, m, (pair, pair, tile, both), (both,), gradient, damping, jacobi_scale
    )
    answer = ()
    for number in range(1, ITERS):
        residual, direction, energy, *answer = phase(
            functools.partial(middle_phase, number > 1), "middle_phase", number, n, m, (pair, pair, tile, one), (),
            product(direction), residual, direction, diag, energy, *answer,
        )
    residual, answer = phase(
        last_phase, "last_phase", ITERS, n, m, (damping.shape, damping.shape), (),
        product(direction), residual, direction, diag, energy, *answer,
    )
    return (answer, residual)


def solution(mesh):
    placed = (
        P(("lm", "kf"), None),
        P(("lm", "kf"), None, None),
        P(("lm", "kf"), None, None),
        P(("lm", "kf"), None),
        P(("lm", "kf")),
        P(None, "kf"),
        P(None, "kf"),
    )
    return jax.shard_map(
        shards,
        mesh=mesh,
        in_specs=placed,
        out_specs=(P(None, "kf"), P(None, "kf")),
        check_vma=False,
    )
```

time: 133 us -> 140 us (1.053)
  Pallas kernels: 117 us -> 130 us
  local copies, waits for them, and re-layouts: 9.74 us -> 5.6 us
  other arithmetic: 2.91 us -> 1.31 us
    pallas_call x3, Pallas kernels: 81.9 us -> 95.5 us  [phase(): pl.pallas_call(functools.partial(kernel, n, m), in_specs=[vmem] * len(ope...]
    slice x3 -> x0, local copies, waits for them, and re-layouts: 3.12 us -> none  [the longest x2 2.06 us: from_groups(): return jnp.moveaxis(array, 0, 1).reshape(PAD, -1)[:state]]
    unnamed x7 -> x3, local copies, waits for them, and re-layouts: 3.11 us -> 4.69 us
    broadcast_in_dim x2 -> x0, local copies, waits for them, and re-layouts: 1.54 us -> none  [the longest x1 0.82 us: product(): held = field if used else jnp.zeros(pair, jnp.float32)]
  transfers between devices with their start and end apart: 1 -> 0, of which waited for: 0 -> 0; matrix products, arithmetic and copies ran while one was open for 5% -> 0% of each run, Pallas kernels for 8% -> 0%
where the time goes in v4:
time: 140 us; the launch traced here: 139 us
  Pallas kernels  130 us (93%)
  local copies, waits for them, and re-layouts  5.6 us (4%)
  matrix products  1.55 us (1%)
    pallas_call x3, Pallas kernels, phase(): pl.pallas_call(functools.partial(kernel, n, m), in_specs=[vmem] * len(ope...  95.5 us
    pallas_call x3, Pallas kernels, local_terms(): pl.pallas_call(functools.partial(local_kernel, use_field), grid_spec=pltp...  34.5 us
    unnamed x3, local copies, waits for them, and re-layouts  4.69 us

profile of v4, /device:TPU:0, one launch (start us, length us, event | category | flops | bytes accessed | tf_op | source)
XLA Modules:
  0.0 139.1 jit_solution(14839203609616278962)
XLA Ops:
  0.7 0.8 broadcast_subtract_fusion
  1.4 0.5 fusion.10.starts
  2.0 1.5 %fusion.code_ref = s32[128,128]{1,0:T(8,128)} fusion(s32[128,64]{0,1:T(8,128)S(1)} %broadcast_subtract_fusion, s32[128]{0:T(128)S(1)} %get-tuple-element.22, s32[128]{0:T(128)S(1)} %get-tuple-element.23, s32[128]{0:T(128)S(1)} %multiply_bitcast_fusion, s32[128]{0:T(128)} %param.11, pred[128]{0:T(512)(128)(4,1)S(1)} %compare_and_fusion), kind=kOutput, calls=%fused_computation.1 | convolution fusion | flops 12664832 | bytes 100480 | tf_op jit(solution)/shard_map/dot_general | solution.py:373
  3.5 1.4 copy.9
  4.9 0.9 pad.4.jac_ref
  5.8 10.6 %local_gradient.1.h = f32[64,16,128]{2,1,0:T(8,128)} custom-call(s32[128]{0:T(128)} %fusion.10.starts, bf16[128,128]{1,0:T(8,128)(2,1)} %field_ref.1, s32[128,128]{1,0:T(8,128)} %fusion.code_ref, bf16[128,16,128]{2,1,0:T(8,128)(2,1)} %pad.4.jac_ref, bf16[128,128,128]{2,1,0:T(8,128)(2,1)} %null_ref.5), custom_call_target="tpu_custom_call" | custom-call | tf_op jit(solution)/shard_map/local_gradient/pallas_call | solution.py:70
  16.3 33.4 %first_phase.1 = (f32[64,16,128]{2,1,0:T(8,128)}, f32[64,16,128]{2,1,0:T(8,128)}, f32[8,128]{1,0:T(8,128)}, f32[64,32,128]{2,1,0:T(8,128)}) custom-call(f32[64,16,128]{2,1,0:T(8,128)} %local_gradient.1.h, f32[15,4096]{1,0:T(8,128)} %damping.1, f32[15,4096]{1,0:T(8,128)} %jacobi_scale.1), custom_call_target="tpu_custom_call" | custom-call | tf_op jit(solution)/shard_map/first_phase/pallas_call | solution.py:342
  49.8 12.0 %local_field.2.h = f32[64,16,128]{2,1,0:T(8,128)} custom-call(s32[128]{0:T(128)} %fusion.10.starts, f32[64,16,128]{2,1,0:T(8,128)} %get-tuple-element.12.field_ref.direction, s32[128,128]{1,0:T(8,128)} %fusion.code_ref, bf16[128,16,128]{2,1,0:T(8,128)(2,1)} %pad.4.jac_ref, bf16[128,128,128]{2,1,0:T(8,128)(2,1)} %null_ref.5), custom_call_target="tpu_custom_call" | custom-call | tf_op jit(solution)/shard_map/local_field/pallas_call | solution.py:70
  61.7 31.1 %middle_phase.1 = (f32[64,16,128]{2,1,0:T(8,128)}, f32[64,16,128]{2,1,0:T(8,128)}, f32[8,128]{1,0:T(8,128)}, f32[32,16,128]{2,1,0:T(8,128)}) custom-call(f32[64,16,128]{2,1,0:T(8,128)} %local_field.2.h, f32[64,16,128]{2,1,0:T(8,128)} %get-tuple-element.13.res, f32[64,16,128]{2,1,0:T(8,128)} %get-tuple-element.12.field_ref.direction, ...), custom_call_target="tpu_custom_call" | custom-call | tf_op jit(solution)/shard_map/middle_phase/pallas_call | solution.py:342
  92.8 12.0 %local_field.3.h = f32[64,16,128]{2,1,0:T(8,128)} custom-call(s32[128]{0:T(128)} %fusion.10.starts, f32[64,16,128]{2,1,0:T(8,128)} %get-tuple-element.16.field_ref.direction, s32[128,128]{1,0:T(8,128)} %fusion.code_ref, bf16[128,16,128]{2,1,0:T(8,128)(2,1)} %pad.4.jac_ref, bf16[128,128,128]{2,1,0:T(8,128)(2,1)} %null_ref.5), custom_call_target="tpu_custom_call" | custom-call | tf_op jit(solution)/shard_map/local_field/pallas_call | solution.py:70
  104.8 30.9 %last_phase.1 = (f32[15,4096]{1,0:T(8,128)}, f32[15,4096]{1,0:T(8,128)}) custom-call(f32[64,16,128]{2,1,0:T(8,128)} %local_field.3.h, f32[64,16,128]{2,1,0:T(8,128)} %get-tuple-element.17.res, f32[64,16,128]{2,1,0:T(8,128)} %get-tuple-element.16.field_ref.direction, f32[64,32,128]{2,1,0:T(8,128)} %get-tuple-element.14.diag, ...), custom_call_target="tpu_custom_call" | custom-call | tf_op jit(solution)/shard_map/last_phase/pallas_call | solution.py:342
  135.8 1.7 %copy.12 = f32[15,4096]{1,0:T(8,128)} copy(f32[15,4096]{1,0:T(8,128)} %get-tuple-element.26) | data formatting | bytes 491520
  137.4 1.7 %copy.13 = f32[15,4096]{1,0:T(8,128)} copy(f32[15,4096]{1,0:T(8,128)} %get-tuple-element.27) | data formatting | bytes 491520
  (3 shorter events, 0.0 us)

commit v5 on v3

--- a/solution.py
+++ b/solution.py
@@ -11,10 +11,10 @@
 LANES = 128
 PAD = 16
 SPAN = 5
-CHUNK = 16
-
-
-def local_kernel(use_field, starts, field_ref, code_ref, res_ref, jac_ref, null_ref, out_ref, hot_ref, row_ref):
+CHUNK = 32
+
+
+def local_kernel(use_field, starts, field_ref, code_ref, jac_ref, null_ref, out_ref, hot_ref, row_ref):
     step = pl.program_id(0)
 
     @pl.when(step == 0)
@@ -38,7 +38,7 @@
             jac = jac_ref[i].astype(jnp.float32)
             row_ref[pl.ds(i, 1), :] = jnp.sum(jac * gathered, axis=0, keepdims=True)
     else:
-        row_ref[...] = jnp.where(code_ref[...] >= 0, res_ref[...], 0.0)
+        row_ref[...] = jnp.where(code_ref[...] >= 0, field_ref[...].astype(jnp.float32), 0.0)
     inner = []
     for i in range(CHUNK):
         lifted = row_ref[pl.ds(i, 1), :].astype(jnp.bfloat16)
@@ -61,17 +61,19 @@
         out_ref[pl.ds(begin[i], SPAN)] += back[i]
 
 
-def local_terms(use_field, starts, field, code, res, jac, null):
+def local_terms(use_field, starts, field, code, jac, null, groups):
     blocks = null.shape[0]
-    groups = field.shape[0]
+    if use_field:
+        source = pl.BlockSpec(field.shape, lambda b, s: (0, 0, 0))
+    else:
+        source = pl.BlockSpec((CHUNK, LANES), lambda b, s: (b, 0))
     return pl.pallas_call(
         functools.partial(local_kernel, use_field),
         grid_spec=pltpu.PrefetchScalarGridSpec(
             num_scalar_prefetch=1,
             grid=(blocks // CHUNK,),
             in_specs=[
-                pl.BlockSpec(field.shape, lambda b, s: (0, 0, 0)),
-                pl.BlockSpec((CHUNK, LANES), lambda b, s: (b, 0)),
+                source,
                 pl.BlockSpec((CHUNK, LANES), lambda b, s: (b, 0)),
                 pl.BlockSpec((CHUNK, PAD, LANES), lambda b, s: (b, 0, 0)),
                 pl.BlockSpec((CHUNK, LANES, LANES), lambda b, s: (b, 0, 0)),
@@ -84,13 +86,7 @@
         ),
         out_shape=jax.ShapeDtypeStruct((groups, PAD, LANES), jnp.float32),
         name="local_field" if use_field else "local_gradient",
-    )(starts, field, code, res, jac, null)
-
-
-def passed_along(array, axis, by):
-    length = lax.axis_size(axis)
-    pairs = [(i, i + by) for i in range(length) if 0 <= i + by < length]
-    return lax.ppermute(array, axis, pairs)
+    )(starts, field, code, jac, null)
 
 
 def remote(src, dst, send, recv, axis, index):
@@ -220,57 +216,96 @@
     return jnp.sum(jnp.sum(total, axis=0, keepdims=True), axis=1, keepdims=True), finish
 
 
-def first_phase(n, m, h, scale, res_out, dir_out, energy_out, full, fold, acc, rs, slots, *sems):
+def columns(g):
+    return pl.ds(g * LANES, LANES)
+
+
+def first_phase(n, m, h, damping, jacobi_scale, res_out, dir_out, energy_out, diag_out, full, fold, acc, rs, slots, diag, *sems):
     own = acc.shape[0]
+    state = damping.shape[0]
+    w = lax.axis_index("kf")
+    diag[...] = jnp.zeros_like(diag)
+    for g in range(own):
+        diag[g, pl.ds(0, state), :] = damping[:, columns(g)]
+        diag[g, pl.ds(PAD, state), :] = jacobi_scale[:, columns(g)]
     greet(n, m)
+    diag_copy = remote(
+        diag.at[pl.ds(0, own)], diag.at[pl.ds(own, own)], sems[10].at[0], sems[10].at[1], "kf", lax.rem(w + m - 1, m)
+    )
+
+    @pl.when(w > 0)
+    def _():
+        diag_copy.start()
+
     finish_pair, finish_sends = reduce_spread(n, m, True, h, full, (fold, acc, rs), sems[:8])
     grad = full[pl.ds(0, own)]
-    energy, finish = over_windows(m, grad * grad * scale[pl.ds(0, own)], slots.at[0], sems[8].at[0], sems[9].at[0])
+    scale = diag[pl.ds(0, own), pl.ds(PAD, PAD), :]
+    energy, finish = over_windows(m, grad * grad * scale, slots.at[0], sems[8].at[0], sems[9].at[0])
     energy_out[...] = jnp.broadcast_to(energy, energy_out.shape)
     finish_pair()
+
+    @pl.when(w < m - 1)
+    def _():
+        diag_copy.wait_recv()
+
+    @pl.when(w > 0)
+    def _():
+        diag_copy.wait_send()
+
     res_out[...] = -full[...]
-    dir_out[...] = -full[...] * scale[...]
+    dir_out[...] = -full[...] * diag[:, pl.ds(PAD, PAD), :]
+    diag_out[...] = diag[...]
     finish()
     finish_sends()
 
 
-def middle_phase(n, m, h, res, direction, scale, damp, energy_in, answer_in, res_out, dir_out, energy_out, answer_out, full, fold, acc, rs, slots, *sems):
+def middle_phase(begun, n, m, h, res, direction, diag, energy_in, *rest):
+    if begun:
+        answer_in, *rest = rest
+    res_out, dir_out, energy_out, answer_out, full, fold, acc, rs, slots, *sems = rest
     own = acc.shape[0]
-    here = pl.ds(0, own)
+    here, damp, scale = pl.ds(0, own), pl.ds(0, PAD), pl.ds(PAD, PAD)
     greet(n, m)
     finish_pair, finish_sends = reduce_spread(n, m, True, h, full, (fold, acc, rs), sems[:8])
     energy = energy_in[pl.ds(0, 1), pl.ds(0, 1)]
-    applied = full[here] + damp[here] * direction[here]
+    applied = full[here] + diag[here, damp, :] * direction[here]
     curve, finish_a = over_windows(m, direction[here] * applied, slots.at[0], sems[8].at[0], sems[9].at[0])
     step = energy / curve
     after = res[here] - step * applied
-    fresh, finish_b = over_windows(m, after * after * scale[here], slots.at[1], sems[8].at[1], sems[9].at[1])
-    answer_out[...] = answer_in[...] + step * direction[here]
+    fresh, finish_b = over_windows(m, after * after * diag[here, scale, :], slots.at[1], sems[8].at[1], sems[9].at[1])
+    gained = step * direction[here]
+    answer_out[...] = answer_in[...] + gained if begun else gained
     energy_out[...] = jnp.broadcast_to(fresh, energy_out.shape)
     finish_pair()
-    after = res[...] - step * (full[...] + damp[...] * direction[...])
+    after = res[...] - step * (full[...] + diag[:, damp, :] * direction[...])
     res_out[...] = after
-    dir_out[...] = scale[...] * after + fresh / energy * direction[...]
+    dir_out[...] = diag[:, scale, :] * after + fresh / energy * direction[...]
     finish_a()
     finish_b()
     finish_sends()
 
 
-def last_phase(n, m, h, res, direction, damp, energy_in, answer_in, res_out, answer_out, full, fold, acc, rs, slots, *sems):
+def last_phase(n, m, h, res, direction, diag, energy_in, answer_in, res_out, applied_out, answer_out, dir_out, step_out, full, fold, acc, rs, slots, *sems):
     own = acc.shape[0]
+    state = res_out.shape[0]
     here = pl.ds(0, own)
     greet(n, m)
+    for g in range(own):
+        res_out[:, columns(g)] = res[g, pl.ds(0, state), :]
+        answer_out[:, columns(g)] = answer_in[g, pl.ds(0, state), :]
+        dir_out[:, columns(g)] = direction[g, pl.ds(0, state), :]
     _, finish_sends = reduce_spread(n, m, False, h, full, (fold, acc, rs), sems[:8])
-    applied = full[here] + damp[here] * direction[here]
+    applied = full[here] + diag[here, pl.ds(0, PAD), :] * direction[here]
     curve, finish = over_windows(m, direction[here] * applied, slots.at[0], sems[8].at[0], sems[9].at[0])
     step = energy_in[pl.ds(0, 1), pl.ds(0, 1)] / curve
-    answer_out[...] = answer_in[...] + step * direction[here]
-    res_out[...] = res[here] - step * applied
+    step_out[...] = jnp.broadcast_to(step, step_out.shape)
+    for g in range(own):
+        applied_out[:, columns(g)] = applied[g, :state]
     finish()
     finish_sends()
 
 
-def phase(kernel, number, n, m, outs, *operands):
+def phase(kernel, name, number, n, m, outs, extra, *operands):
     pair = operands[0].shape
     own = pair[0] // 2
     tile = pair[1:]
@@ -288,21 +323,13 @@
             pltpu.VMEM((n, own // n) + tile, jnp.float32),
             pltpu.VMEM((2, m) + tile, jnp.float32),
         ]
+        + [pltpu.VMEM(shape, jnp.float32) for shape in extra]
         + [dma((n,))] * 8
-        + [dma((2, m))] * 2,
+        + [dma((2, m))] * 2
+        + [dma((2,))],
         compiler_params=pltpu.CompilerParams(collective_id=number, has_side_effects=True),
-        name=kernel.__name__,
+        name=name,
     )(*operands)
-
-
-def to_groups(array):
-    state, frames = array.shape
-    padded = jnp.pad(array, ((0, PAD - state), (0, 0)))
-    return jnp.moveaxis(padded.reshape(PAD, frames // LANES, LANES), 1, 0)
-
-
-def from_groups(array, state):
-    return jnp.moveaxis(array, 0, 1).reshape(PAD, -1)[:state]
 
 
 def prepare(frame_ids, obs_count, first_frame, groups):
@@ -323,29 +350,29 @@
     own = frames // LANES
     starts, code = prepare(frame_ids, obs_count, lax.axis_index("kf") * frames, 2 * own)
     jac = jnp.pad(jacobian, ((0, 0), (0, PAD - state), (0, 0)))
-    res = residual_rows.astype(jnp.float32)
     n, m = lax.axis_size("lm"), lax.axis_size("kf")
-    window = jnp.concatenate([to_groups(damping), to_groups(jacobi_scale)], axis=1)
-    window = jnp.concatenate([window, passed_along(window, "kf", -1)], axis=0)
-    damp, scale = window[:, :PAD], window[:, PAD:]
     pair, one, tile = (2 * own, PAD, LANES), (own, PAD, LANES), (8, LANES)
+    both = (2 * own, 2 * PAD, LANES)
 
     def product(field):
-        used = field is not None
-        held = field if used else jnp.zeros(pair, jnp.float32)
-        return local_terms(used, starts, held, code, res, jac, nullspace)
-
-    residual, direction, energy = phase(first_phase, 0, n, m, (pair, pair, tile), product(None), scale)
-    answer = jnp.zeros(one, jnp.float32)
+        return local_terms(True, starts, field, code, jac, nullspace, 2 * own)
+
+    gradient = local_terms(False, starts, residual_rows, code, jac, nullspace, 2 * own)
+    residual, direction, energy, diag = phase(
+        first_phase, "first_phase", 0, n, m, (pair, pair, tile, both), (both,), gradient, damping, jacobi_scale
+    )
+    answer = ()
     for number in range(1, ITERS):
-        residual, direction, energy, answer = phase(
-            middle_phase, number, n, m, (pair, pair, tile, one),
-            product(direction), residual, direction, scale, damp, energy, answer,
+        residual, direction, energy, *answer = phase(
+            functools.partial(middle_phase, number > 1), "middle_phase", number, n, m, (pair, pair, tile, one), (),
+            product(direction), residual, direction, diag, energy, *answer,
         )
-    residual, answer = phase(
-        last_phase, ITERS, n, m, (one, one), product(direction), residual, direction, damp, energy, answer
-    )
-    return (from_groups(answer, state), from_groups(residual, state))
+    residual, applied, answer, direction, step = phase(
+        last_phase, "last_phase", ITERS, n, m, (damping.shape,) * 4 + (tile,), (),
+        product(direction), residual, direction, diag, energy, *answer,
+    )
+    step = step[0, 0]
+    return (answer + step * direction, residual - step * applied)
 
 
 def solution(mesh):

time: 133 us -> 127 us (0.955)
  local copies, waits for them, and re-layouts: 9.74 us -> 3.48 us
  other arithmetic: 2.91 us -> 6.04 us
  Pallas kernels: 117 us -> 115 us
    add x0 -> x1, other arithmetic: none -> 2.37 us  [shards(): return (answer + step * direction, residual - step * applied)]
    sub x0 -> x1, other arithmetic: none -> 2.37 us  [shards(): return (answer + step * direction, residual - step * applied)]
    pallas_call x3, Pallas kernels: 34.7 us -> 32.8 us  [local_terms(): pl.pallas_call(functools.partial(local_kernel, use_field), grid_spec=pltp...]
    slice x3 -> x1, local copies, waits for them, and re-layouts: 3.12 us -> 1.22 us  [shards(): step = step[0, 0]]
    unnamed x7 -> x1, local copies, waits for them, and re-layouts: 3.11 us -> 1.35 us
    broadcast_in_dim x2 -> x0, local copies, waits for them, and re-layouts: 1.54 us -> none  [the longest x1 0.82 us: product(): held = field if used else jnp.zeros(pair, jnp.float32)]
    convert_element_type x1 -> x0, other arithmetic: 1.38 us -> none  [shards(): res = residual_rows.astype(jnp.float32)]
  transfers between devices with their start and end apart: 1 -> 0, of which waited for: 0 -> 0; matrix products, arithmetic and copies ran while one was open for 5% -> 0% of each run, Pallas kernels for 8% -> 0%
where the time goes in v5:
time: 127 us
  Pallas kernels  115 us (91%)
  other arithmetic  6.04 us (5%)
  local copies, waits for them, and re-layouts  3.48 us (3%)
  matrix products  1.55 us (1%)
    pallas_call x3, Pallas kernels, phase(): pl.pallas_call(functools.partial(kernel, n, m), in_specs=[vmem] * len(ope...  82.1 us
    pallas_call x3, Pallas kernels, local_terms(): pl.pallas_call(functools.partial(local_kernel, use_field), grid_spec=pltp...  32.8 us

profile of v5, /device:TPU:0, one launch (start us, length us, event | category | flops | bytes accessed | tf_op | source)
XLA Modules:
  0.0 126.6 jit_solution(16373903075260725429)
XLA Ops:
  0.7 0.8 broadcast_subtract_fusion
  1.4 0.5 fusion.10.starts
  2.0 1.5 %fusion.code_ref = s32[128,128]{1,0:T(8,128)} fusion(s32[128,64]{0,1:T(8,128)S(1)} %broadcast_subtract_fusion, s32[128]{0:T(128)S(1)} %get-tuple-element.28, s32[128]{0:T(128)S(1)} %get-tuple-element.29, s32[128]{0:T(128)S(1)} %multiply_bitcast_fusion, s32[128]{0:T(128)} %param.11, pred[128]{0:T(512)(128)(4,1)S(1)} %compare_and_fusion), kind=kOutput, calls=%fused_computation.1 | convolution fusion | flops 12664832 | bytes 100480 | tf_op jit(solution)/shard_map/dot_general | solution.py:344
  3.5 1.4 %copy.9 = bf16[128,15,128]{2,1,0:T(8,128)(2,1)S(1)} copy(bf16[128,15,128]{2,0,1:T(8,128)(2,1)} %param.8) | data formatting | bytes 983040 | tf_op args[1]
  4.9 0.9 pad.4.jac_ref
  5.8 9.6 %local_gradient.1.h = f32[64,16,128]{2,1,0:T(8,128)} custom-call(s32[128]{0:T(128)} %fusion.10.starts, bf16[128,128]{1,0:T(8,128)(2,1)} %field_ref.1, s32[128,128]{1,0:T(8,128)} %fusion.code_ref, bf16[128,16,128]{2,1,0:T(8,128)(2,1)} %pad.4.jac_ref, bf16[128,128,128]{2,1,0:T(8,128)(2,1)} %null_ref.5), custom_call_target="tpu_custom_call" | custom-call | tf_op jit(solution)/shard_map/local_gradient/pallas_call | solution.py:70
  15.4 29.0 %first_phase.1 = (f32[64,16,128]{2,1,0:T(8,128)}, f32[64,16,128]{2,1,0:T(8,128)}, f32[8,128]{1,0:T(8,128)}, f32[64,32,128]{2,1,0:T(8,128)}) custom-call(f32[64,16,128]{2,1,0:T(8,128)} %local_gradient.1.h, f32[15,4096]{1,0:T(8,128)} %damping.1, f32[15,4096]{1,0:T(8,128)} %jacobi_scale.1), custom_call_target="tpu_custom_call" | custom-call | tf_op jit(solution)/shard_map/first_phase/pallas_call | solution.py:314
  44.4 11.6 %local_field.2.h = f32[64,16,128]{2,1,0:T(8,128)} custom-call(s32[128]{0:T(128)} %fusion.10.starts, f32[64,16,128]{2,1,0:T(8,128)} %get-tuple-element.15.field_ref.direction, s32[128,128]{1,0:T(8,128)} %fusion.code_ref, bf16[128,16,128]{2,1,0:T(8,128)(2,1)} %pad.4.jac_ref, bf16[128,128,128]{2,1,0:T(8,128)(2,1)} %null_ref.5), custom_call_target="tpu_custom_call" | custom-call | tf_op jit(solution)/shard_map/local_field/pallas_call | solution.py:70
  56.0 28.7 %middle_phase.1 = (f32[64,16,128]{2,1,0:T(8,128)}, f32[64,16,128]{2,1,0:T(8,128)}, f32[8,128]{1,0:T(8,128)}, f32[32,16,128]{2,1,0:T(8,128)}) custom-call(f32[64,16,128]{2,1,0:T(8,128)} %local_field.2.h, f32[64,16,128]{2,1,0:T(8,128)} %get-tuple-element.16.res, f32[64,16,128]{2,1,0:T(8,128)} %get-tuple-element.15.field_ref.direction, ...), custom_call_target="tpu_custom_call" | custom-call | tf_op jit(solution)/shard_map/middle_phase/pallas_call | solution.py:314
  84.7 11.6 %local_field.3.h = f32[64,16,128]{2,1,0:T(8,128)} custom-call(s32[128]{0:T(128)} %fusion.10.starts, f32[64,16,128]{2,1,0:T(8,128)} %get-tuple-element.19.field_ref.direction, s32[128,128]{1,0:T(8,128)} %fusion.code_ref, bf16[128,16,128]{2,1,0:T(8,128)(2,1)} %pad.4.jac_ref, bf16[128,128,128]{2,1,0:T(8,128)(2,1)} %null_ref.5), custom_call_target="tpu_custom_call" | custom-call | tf_op jit(solution)/shard_map/local_field/pallas_call | solution.py:70
  96.3 24.4 %last_phase.1 = (f32[15,4096]{1,0:T(8,128)}, f32[15,4096]{1,0:T(8,128)}, f32[15,4096]{1,0:T(8,128)}, f32[15,4096]{1,0:T(8,128)}, f32[8,128]{1,0:T(8,128)}) custom-call(f32[64,16,128]{2,1,0:T(8,128)} %local_field.3.h, f32[64,16,128]{2,1,0:T(8,128)} %get-tuple-element.20.res, f32[64,16,128]{2,1,0:T(8,128)} %get-tuple-element.19.field_ref.direction, ...), custom_call_target="tpu_custom_call" | custom-call | tf_op jit(solution)/shard_map/last_phase/pallas_call | solution.py:314
  120.7 1.2 slice.7
  121.9 2.4 %multiply_add_fusion = f32[15,4096]{1,0:T(8,128)} fusion(f32[15,4096]{1,0:T(8,128)} %get-tuple-element.23, f32[15,4096]{1,0:T(8,128)} %get-tuple-element.25, f32[]{:T(128)} %bitcast.2), kind=kLoop, calls=%fused_computation.3 | loop fusion | flops 122880 | bytes 737284 | tf_op jit(solution)/shard_map/add | solution.py:375
  124.3 2.4 %multiply_subtract_fusion = f32[15,4096]{1,0:T(8,128)} fusion(f32[15,4096]{1,0:T(8,128)} %get-tuple-element.26, f32[15,4096]{1,0:T(8,128)} %get-tuple-element.27, f32[]{:T(128)} %bitcast.2), kind=kLoop, calls=%fused_computation.2 | loop fusion | flops 122880 | bytes 737284 | tf_op jit(solution)/shard_map/sub | solution.py:375
  (3 shorter events, 0.0 us)

commit v6 on v5

--- a/solution.py
+++ b/solution.py
@@ -285,24 +285,40 @@
     finish_sends()
 
 
-def last_phase(n, m, h, res, direction, diag, energy_in, answer_in, res_out, applied_out, answer_out, dir_out, step_out, full, fold, acc, rs, slots, *sems):
+def last_phase(n, m, h, direction, diag, energy_in, applied_out, step_out, full, fold, acc, rs, slots, *sems):
     own = acc.shape[0]
-    state = res_out.shape[0]
     here = pl.ds(0, own)
     greet(n, m)
-    for g in range(own):
-        res_out[:, columns(g)] = res[g, pl.ds(0, state), :]
-        answer_out[:, columns(g)] = answer_in[g, pl.ds(0, state), :]
-        dir_out[:, columns(g)] = direction[g, pl.ds(0, state), :]
     _, finish_sends = reduce_spread(n, m, False, h, full, (fold, acc, rs), sems[:8])
     applied = full[here] + diag[here, pl.ds(0, PAD), :] * direction[here]
+    applied_out[...] = applied
     curve, finish = over_windows(m, direction[here] * applied, slots.at[0], sems[8].at[0], sems[9].at[0])
     step = energy_in[pl.ds(0, 1), pl.ds(0, 1)] / curve
     step_out[...] = jnp.broadcast_to(step, step_out.shape)
-    for g in range(own):
-        applied_out[:, columns(g)] = applied[g, :state]
     finish()
     finish_sends()
+
+
+def update_kernel(res, direction, applied, answer_in, step_in, answer_out, res_out):
+    own = applied.shape[0]
+    state = res_out.shape[0]
+    step = step_in[pl.ds(0, 1), pl.ds(0, 1)]
+    for g in range(own):
+        answer_out[:, columns(g)] = (answer_in[g] + step * direction[g])[:state]
+        res_out[:, columns(g)] = (res[g] - step * applied[g])[:state]
+
+
+def last_update(shape, res, direction, applied, answer, step):
+    half = pl.BlockSpec(applied.shape, lambda i: (0, 0, 0))
+    whole = pl.BlockSpec(shape, lambda i: (0, 0))
+    return pl.pallas_call(
+        update_kernel,
+        grid=(1,),
+        in_specs=[half] * 4 + [pl.BlockSpec(step.shape, lambda i: (0, 0))],
+        out_specs=[whole] * 2,
+        out_shape=[jax.ShapeDtypeStruct(shape, jnp.float32)] * 2,
+        name="last_update",
+    )(res, direction, applied, answer, step)
 
 
 def phase(kernel, name, number, n, m, outs, extra, *operands):
@@ -367,12 +383,10 @@
             functools.partial(middle_phase, number > 1), "middle_phase", number, n, m, (pair, pair, tile, one), (),
             product(direction), residual, direction, diag, energy, *answer,
         )
-    residual, applied, answer, direction, step = phase(
-        last_phase, "last_phase", ITERS, n, m, (damping.shape,) * 4 + (tile,), (),
-        product(direction), residual, direction, diag, energy, *answer,
-    )
-    step = step[0, 0]
-    return (answer + step * direction, residual - step * applied)
+    applied, step = phase(
+        last_phase, "last_phase", ITERS, n, m, (one, tile), (), product(direction), direction, diag, energy
+    )
+    return tuple(last_update(damping.shape, residual, direction, applied, *answer, step))
 
 
 def solution(mesh):

time: 127 us -> 123 us (0.969)
  other arithmetic: 6.04 us -> 1.31 us
    add x1 -> x0, other arithmetic: 2.37 us -> none  [shards(): return (answer + step * direction, residual - step * applied)]
    sub x1 -> x0, other arithmetic: 2.37 us -> none  [shards(): return (answer + step * direction, residual - step * applied)]
    pallas_call x0 -> x1, Pallas kernels: none -> 2.06 us  [last_update(): pl.pallas_call(update_kernel, grid=(1,), in_specs=[half] * 4 + [pl.BlockS...]
where the time goes in v6:
time: 123 us; the launch traced here: 122 us
  Pallas kernels  116 us (94%)
  local copies, waits for them, and re-layouts  2.26 us (2%)
  matrix products  1.55 us (1%)
  other arithmetic  1.31 us (1%)
    pallas_call x3, Pallas kernels, phase(): pl.pallas_call(functools.partial(kernel, n, m), in_specs=[vmem] * len(ope...  81.7 us
    pallas_call x3, Pallas kernels, local_terms(): pl.pallas_call(functools.partial(local_kernel, use_field), grid_spec=pltp...  32.7 us

profile of v6, /device:TPU:0, one launch (start us, length us, event | category | flops | bytes accessed | tf_op | source)
XLA Modules:
  0.0 122.3 jit_solution(6896648907478622695)
XLA Ops:
  0.7 0.8 broadcast_subtract_fusion
  1.4 0.5 fusion.10.starts
  2.0 1.5 %fusion.code_ref = s32[128,128]{1,0:T(8,128)} fusion(s32[128,64]{0,1:T(8,128)S(1)} %broadcast_subtract_fusion, s32[128]{0:T(128)S(1)} %get-tuple-element.22, s32[128]{0:T(128)S(1)} %get-tuple-element.23, s32[128]{0:T(128)S(1)} %multiply_bitcast_fusion, s32[128]{0:T(128)} %param.11, pred[128]{0:T(512)(128)(4,1)S(1)} %compare_and_fusion), kind=kOutput, calls=%fused_computation.1 | convolution fusion | flops 12664832 | bytes 100480 | tf_op jit(solution)/shard_map/dot_general | solution.py:360
  3.5 1.4 %copy.9 = bf16[128,15,128]{2,1,0:T(8,128)(2,1)S(1)} copy(bf16[128,15,128]{2,0,1:T(8,128)(2,1)} %param.8) | data formatting | bytes 983040 | tf_op args[1]
  4.9 0.9 pad.4.jac_ref
  5.8 9.6 %local_gradient.1.h = f32[64,16,128]{2,1,0:T(8,128)} custom-call(s32[128]{0:T(128)} %fusion.10.starts, bf16[128,128]{1,0:T(8,128)(2,1)} %field_ref.1, s32[128,128]{1,0:T(8,128)} %fusion.code_ref, bf16[128,16,128]{2,1,0:T(8,128)(2,1)} %pad.4.jac_ref, bf16[128,128,128]{2,1,0:T(8,128)(2,1)} %null_ref.5), custom_call_target="tpu_custom_call" | custom-call | tf_op jit(solution)/shard_map/local_gradient/pallas_call | solution.py:70
  15.4 29.0 %first_phase.1 = (f32[64,16,128]{2,1,0:T(8,128)}, f32[64,16,128]{2,1,0:T(8,128)}, f32[8,128]{1,0:T(8,128)}, f32[64,32,128]{2,1,0:T(8,128)}) custom-call(f32[64,16,128]{2,1,0:T(8,128)} %local_gradient.1.h, f32[15,4096]{1,0:T(8,128)} %damping.1, f32[15,4096]{1,0:T(8,128)} %jacobi_scale.1), custom_call_target="tpu_custom_call" | custom-call | tf_op jit(solution)/shard_map/first_phase/pallas_call | solution.py:330
  44.4 11.6 %local_field.2.h = f32[64,16,128]{2,1,0:T(8,128)} custom-call(s32[128]{0:T(128)} %fusion.10.starts, f32[64,16,128]{2,1,0:T(8,128)} %get-tuple-element.12.field_ref.direction, s32[128,128]{1,0:T(8,128)} %fusion.code_ref, bf16[128,16,128]{2,1,0:T(8,128)(2,1)} %pad.4.jac_ref, bf16[128,128,128]{2,1,0:T(8,128)(2,1)} %null_ref.5), custom_call_target="tpu_custom_call" | custom-call | tf_op jit(solution)/shard_map/local_field/pallas_call | solution.py:70
  56.0 28.7 %middle_phase.1 = (f32[64,16,128]{2,1,0:T(8,128)}, f32[64,16,128]{2,1,0:T(8,128)}, f32[8,128]{1,0:T(8,128)}, f32[32,16,128]{2,1,0:T(8,128)}) custom-call(f32[64,16,128]{2,1,0:T(8,128)} %local_field.2.h, f32[64,16,128]{2,1,0:T(8,128)} %get-tuple-element.13.res, f32[64,16,128]{2,1,0:T(8,128)} %get-tuple-element.12.field_ref.direction, ...), custom_call_target="tpu_custom_call" | custom-call | tf_op jit(solution)/shard_map/middle_phase/pallas_call | solution.py:330
  84.7 11.6 %local_field.3.h = f32[64,16,128]{2,1,0:T(8,128)} custom-call(s32[128]{0:T(128)} %fusion.10.starts, f32[64,16,128]{2,1,0:T(8,128)} %get-tuple-element.17.field_ref.direction, s32[128,128]{1,0:T(8,128)} %fusion.code_ref, bf16[128,16,128]{2,1,0:T(8,128)(2,1)} %pad.4.jac_ref, bf16[128,128,128]{2,1,0:T(8,128)(2,1)} %null_ref.5), custom_call_target="tpu_custom_call" | custom-call | tf_op jit(solution)/shard_map/local_field/pallas_call | solution.py:70
  96.3 23.9 %last_phase.1 = (f32[32,16,128]{2,1,0:T(8,128)}, f32[8,128]{1,0:T(8,128)}) custom-call(f32[64,16,128]{2,1,0:T(8,128)} %local_field.3.h, f32[64,16,128]{2,1,0:T(8,128)} %get-tuple-element.17.field_ref.direction, f32[64,32,128]{2,1,0:T(8,128)} %get-tuple-element.14.diag, f32[8,128]{1,0:T(8,128)} %get-tuple-element.18.energy_in), custom_call_target="tpu_custom_call" | custom-call | tf_op jit(solution)/shard_map/last_phase/pallas_call | solution.py:330
  120.2 2.1 %last_update.1 = (f32[15,4096]{1,0:T(8,128)}, f32[15,4096]{1,0:T(8,128)}) custom-call(f32[64,16,128]{2,1,0:T(8,128)} %get-tuple-element.16.res, f32[64,16,128]{2,1,0:T(8,128)} %get-tuple-element.17.field_ref.direction, f32[32,16,128]{2,1,0:T(8,128)} %get-tuple-element.19.applied, f32[32,16,128]{2,1,0:T(8,128)} %get-tuple-element.20.answer_in, ...), custom_call_target="tpu_custom_call" | custom-call | tf_op jit(solution)/shard_map/last_update/pallas_call | solution.py:314
  (3 shorter events, 0.0 us)
